TPU v7x, 32 devices: a whole 2x2x4 slice. The times are simulated.
32 devices in a mesh: group: 2 (over x), branch: 8 (over z, y), expert: 2 (over core).
Axes of the slice: x: 2, y: 2, z: 4, core: 2. Of those that a mesh axis runs over, the one named last changes fastest.
Arguments:
- latent_cache: bfloat16 [16, 2048, 512], P(('group', 'branch'), 'expert'), parts along dimension 0, may hold values from -4 to 4
- rope_cache: bfloat16 [16, 256, 512], P(('group', 'branch'), 'expert'), parts along dimension 0, may hold values from -4 to 4
- q_latent: bfloat16 [256, 2, 128, 512], P(('group', 'branch', 'expert')), parts along dimension 0, may hold values from -4.8 to 4.8
- q_rope: bfloat16 [256, 2, 8192], P(('group', 'branch', 'expert')), parts along dimension 0, may hold values from -192 to 192
- new_latent: bfloat16 [256, 2, 512], P(('group', 'branch', 'expert')), parts along dimension 0, may hold values from -4 to 4
- new_rope: bfloat16 [256, 2, 64], P(('group', 'branch', 'expert')), parts along dimension 0, may hold values from -4.2 to 4.2
- branch_slot: int32 [256], P(('group', 'branch', 'expert')), parts along dimension 0, may hold values from 0 to 7, as said below
- moe_input: bfloat16 [256, 2, 7168], P(('group', 'branch', 'expert')), parts along dimension 0, may hold values from -6 to 6
- routes: int32 [256, 2, 8], P(('group', 'branch', 'expert')), parts along dimension 0, may hold values from 0 to 255, as said below
- route_gate: float32 [256, 2, 8], P(('group', 'branch', 'expert')), parts along dimension 0, may hold values from 0.05 to 0.6
- w_gate: bfloat16 [16, 7168, 128], P(('branch', 'expert')), may hold values from -0.0625 to 0.0625
- w_up: bfloat16 [16, 7168, 128], P(('branch', 'expert')), may hold values from -0.0625 to 0.0625
- w_down: bfloat16 [16, 128, 7168], P(('branch', 'expert')), may hold values from -0.1875 to 0.1875
Outputs:
- attended: bfloat16 [256, 2, 128, 512], P(('group', 'branch', 'expert')), parts along dimension 0
- moe_out: bfloat16 [256, 2, 7168], P(('group', 'branch', 'expert')), parts along dimension 0
There are 2 independent parts, one for each index of `group`. A program takes and returns all parts, laid end to end along the dimension named above; an argument that names none is the same for every part. Nothing has to cross between parts.
Inputs may be any that keep to these rules, and one draw needn't show every extreme that they name: `branch_slot`: among the 8 tokens of one device every number from 0 to 7 stands exactly once. `routes`: each row (a token at a step) names 8 different experts, at most one of them below 2; within the 16 rows of one device no expert below 2 is named more than 2 times, and some one exactly 2 times.
All inputs are finite; a program needn't handle non-finite values.
Results may differ from a plain program's by a relative error of at most 0.0057.
Values may be sent and summed in bfloat16 or wider, within the bound.
A program may use at most 192 MiB of HBM per device.

v0:
```python
import jax
import jax.numpy as jnp
from jax import lax
from jax.sharding import PartitionSpec as P

SHARDS = 8
CAP = 2


softmax_scale = 192.0 ** (-0.5)


def swapped(x, axis, bit):
    return lax.ppermute(x, axis, [(i, i ^ 1 << bit) for i in range(lax.axis_size(axis))])


def partial_softmax(query_lat, query_rope, keys_lat, keys_rope):
    scores = jnp.einsum("omshc,opc->omshp", query_lat, keys_lat, preferred_element_type=jnp.float32)
    scores = scores + jnp.einsum(
        "omshr,opr->omshp", query_rope, keys_rope, preferred_element_type=jnp.float32
    )
    scores = scores * softmax_scale
    cache_peak = jnp.max(scores, axis=-1)
    exponent = jnp.exp(scores - cache_peak[..., None])
    totals = jnp.sum(exponent, axis=-1)
    weights = exponent.astype(jnp.bfloat16)
    summed = jnp.einsum("omshp,opc->omshc", weights, keys_lat, preferred_element_type=jnp.float32)
    cache_out = (summed / totals[..., None]).astype(jnp.bfloat16)
    cache_lse = cache_peak + jnp.log(totals)
    return (cache_out, cache_lse)


def split_half(source, stride):
    pieces = source.reshape((source.shape[0] // (2 * stride), 2, stride) + source.shape[1:])
    return (pieces[:, 0], pieces[:, 1])


def join_half(staying, arrived):
    return jnp.stack([staying, arrived], axis=1).reshape((-1,) + staying.shape[2:])


def on_device(
    latent_cache,
    rope_cache,
    q_latent,
    q_rope,
    new_latent,
    new_rope,
    branch_slot,
    moe_input,
    routes,
    route_gate,
    w_gate,
    w_up,
    w_down,
):
    tok_rows = q_latent.shape[0]
    step_count = q_latent.shape[1]
    head_count = q_latent.shape[2]
    rope_width = new_rope.shape[-1]
    rounds = tok_rows.bit_length() - 1
    lowest = lax.axis_index("expert") == 0
    rope_query = q_rope.reshape(tok_rows, step_count, head_count, rope_width)
    counting = jnp.arange(tok_rows, dtype=jnp.int32)
    other_lat, other_rope = swapped((latent_cache[0], rope_cache[0]), "expert", 0)
    full_lat = jnp.where(
        lowest,
        jnp.concatenate([latent_cache[0], other_lat]),
        jnp.concatenate([other_lat, latent_cache[0]]),
    )[None]
    full_rope = jnp.where(
        lowest,
        jnp.concatenate([rope_cache[0], other_rope]),
        jnp.concatenate([other_rope, rope_cache[0]]),
    )
    full_rope = full_rope.reshape(1, -1, rope_width)
    own_index = lax.axis_index("branch") % tok_rows
    target = jnp.bitwise_xor(own_index, branch_slot)
    chooser = (target[None, :] == counting[:, None]).astype(jnp.int32)
    ordering = jnp.sum(chooser * counting[None, :], axis=1)
    query_lat = jnp.take(q_latent, ordering, axis=0)
    query_rope = jnp.take(q_rope, ordering, axis=0)
    for bit_number in range(rounds):
        stride = 1 << bit_number
        staying_lat, leaving_lat = split_half(query_lat, stride)
        staying_rope, leaving_rope = split_half(query_rope, stride)
        arrived_lat, arrived_rope = swapped((leaving_lat, leaving_rope), "branch", bit_number)
        query_lat = join_half(staying_lat, arrived_lat)
        query_rope = join_half(staying_rope, arrived_rope)
    query_rope = query_rope.reshape(tok_rows, step_count, head_count, rope_width)
    cache_out, cache_lse = partial_softmax(query_lat[None], query_rope[None], full_lat, full_rope)
    cache_out, cache_lse = (cache_out[0], cache_lse[0])
    for bit_number in range(rounds):
        stride = 1 << bit_number
        staying_out, leaving_out = split_half(cache_out, stride)
        staying_lse, leaving_lse = split_half(cache_lse, stride)
        arrived_out, arrived_lse = (
            swapped(leaving_out.astype(jnp.float32), "branch", bit_number).astype(
                leaving_out.dtype
            ),
            swapped(leaving_lse, "branch", bit_number),
        )
        cache_out = join_half(staying_out, arrived_out)
        cache_lse = join_half(staying_lse, arrived_lse)
    cache_out = jnp.take(cache_out, target, axis=0)
    cache_lse = jnp.take(cache_lse, target, axis=0)
    own_scores = jnp.einsum(
        "rshc,rjc->rshj", q_latent, new_latent, preferred_element_type=jnp.float32
    )
    own_scores = own_scores + jnp.einsum(
        "rshp,rjp->rshj", rope_query, new_rope, preferred_element_type=jnp.float32
    )
    own_scores = own_scores * softmax_scale
    causal = (jnp.arange(step_count)[None, :] <= jnp.arange(step_count)[:, None])[None, :, None, :]
    own_peak = jnp.max(jnp.where(causal, own_scores, -1e30), axis=-1)
    own_weight = jnp.where(causal, jnp.exp(own_scores - own_peak[..., None]), 0.0)
    own_total = jnp.sum(own_weight, axis=-1)
    own_sum = jnp.einsum(
        "rshj,rjc->rshc",
        own_weight,
        new_latent.astype(jnp.float32),
        precision=lax.Precision.HIGHEST,
    )
    top_value = jnp.maximum(cache_lse, own_peak)
    factor = jnp.exp(cache_lse - top_value)
    own_factor = jnp.exp(own_peak - top_value)
    numerator = factor[..., None] * cache_out.astype(jnp.float32) + own_factor[..., None] * own_sum
    denominator = factor + own_factor * own_total
    attended = (numerator / denominator[..., None]).astype(jnp.bfloat16)
    model_width = moe_input.shape[-1]
    top_count = routes.shape[-1]
    tok_total = tok_rows * step_count
    expert_count = lax.axis_size("branch") * lax.axis_size("expert") // SHARDS
    capacity = CAP
    flat_routes = routes.reshape(-1)
    inside = flat_routes < expert_count
    onehot = (flat_routes[:, None] == jnp.arange(expert_count, dtype=jnp.int32)[None, :]).astype(
        jnp.int32
    )
    before = jnp.cumsum(onehot, axis=0) - onehot
    position = jnp.sum(before * onehot, axis=1)
    slot_index = jnp.where(inside, flat_routes * capacity + position, -1)
    placing = (
        slot_index[None, :] == jnp.arange(expert_count * capacity, dtype=jnp.int32)[:, None]
    ).astype(jnp.float32)
    placing = jnp.sum(
        placing.reshape(expert_count * capacity, tok_total, top_count), axis=-1
    ).astype(jnp.bfloat16)
    tokens_flat = moe_input.reshape(tok_total, model_width)
    outgoing = jnp.dot(placing, tokens_flat, preferred_element_type=jnp.float32).astype(
        jnp.bfloat16
    )
    outgoing = outgoing.reshape(expert_count, 1, capacity, model_width)
    copies = jnp.broadcast_to(outgoing, (expert_count, SHARDS, capacity, model_width))
    copies = copies.reshape(expert_count * SHARDS, capacity, model_width)
    arrived = lax.all_to_all(copies, ("branch", "expert"), split_axis=0, concat_axis=0, tiled=True)
    flattened = arrived.reshape(-1, model_width)
    gate_value = jnp.dot(flattened, w_gate[0], preferred_element_type=jnp.float32)
    lifted = jnp.dot(flattened, w_up[0], preferred_element_type=jnp.float32)
    hidden = (jax.nn.silu(gate_value) * lifted).astype(jnp.bfloat16)
    returned = lax.all_to_all(
        jnp.dot(hidden, w_down[0], preferred_element_type=jnp.float32)
        .astype(jnp.bfloat16)
        .reshape(arrived.shape),
        ("branch", "expert"),
        split_axis=0,
        concat_axis=0,
        tiled=True,
    )
    expert_sums = jnp.sum(
        returned.reshape(expert_count, SHARDS, capacity, model_width).astype(jnp.float32), axis=1
    )
    expert_sums = expert_sums.reshape(expert_count * capacity, model_width)
    safe_index = jnp.maximum(slot_index, 0)
    picked = jnp.take(expert_sums, safe_index, axis=0).reshape(tok_total, top_count, model_width)
    gate_used = jnp.where(inside, route_gate.reshape(-1), 0.0).reshape(tok_total, top_count, 1)
    combined = jnp.sum(gate_used * picked, axis=1)
    moe_out = combined.astype(jnp.bfloat16).reshape(tok_rows, step_count, model_width)
    return (attended, moe_out)


def solution(mesh):
    return jax.shard_map(
        on_device,
        mesh=mesh,
        in_specs=(
            P(("group", "branch"), "expert", None),
            P(("group", "branch"), "expert", None),
            P(("group", "branch", "expert"), None, None, None),
            P(("group", "branch", "expert"), None, None),
            P(("group", "branch", "expert"), None, None),
            P(("group", "branch", "expert"), None, None),
            P(("group", "branch", "expert")),
            P(("group", "branch", "expert"), None, None),
            P(("group", "branch", "expert"), None, None),
            P(("group", "branch", "expert"), None, None),
            P(("branch", "expert"), None, None),
            P(("branch", "expert"), None, None),
            P(("branch", "expert"), None, None),
        ),
        out_specs=(
            P(("group", "branch", "expert"), None, None, None),
            P(("group", "branch", "expert"), None, None),
        ),
        check_vma=False,
    )
```

profile of v0, /device:TPU:0, one launch (start us, length us, event | category | flops | bytes accessed | tf_op | source)
XLA Modules:
  0.0 287.4 jit_solution(16954718998658454671)
XLA Ops:
  0.7 1.3 compare_and_fusion.2
  2.5 2.0 gather_fusion.3
  4.5 1.9 broadcast_select_fusion
  7.5 3.0 %collective-permute-start = (bf16[4,1,2,128,512]{4,3,2,0,1:T(8,128)(2,1)}, bf16[4,1,2,128,512]{4,3,2,0,1:T(8,128)(2,1)}, u32[]{:S(2)}, u32[]{:S(2)}) collective-permute-start(bf16[4,1,2,128,512]{4,3,2,0,1:T(8,128)(2,1)} %get-tuple-element.21), channel_id=1, source_target_pairs={{0,2},{2,0},{4,6},{6,4},{8,10},{10,8},{12,14},{14,12},{1,3},{3,1},... | collective-permute-start | bytes 3145736 | tf_op jit(solution)/shard_map/ppermute | solution.py:14
  10.6 1.8 gather_fusion
  16.3 1.4 fusion.36
  17.7 1.6 reduce_window_sum.11
  19.3 1.6 select_reduce_fusion
  21.6 1.3 lt.65
  25.5 1.7 reshape.359
  27.2 1.7 convolution_convert_fusion.1
  29.0 1.5 broadcast_in_dim.105
  30.4 1.8 broadcast_in_dim.106
  32.2 6.5 %all-to-all-start = ((bf16[16,2,7168]{2,1,0:T(2,128)(2,1)}), bf16[16,2,7168]{2,1,0:T(2,128)(2,1)}, u32[]{:S(2)}, u32[]{:S(2)}) async-start(bf16[16,2,7168]{2,1,0:T(2,128)(2,1)} %bitcast.168), calls=%async_computation | async-start | bytes 917504 | tf_op jit(solution)/shard_map/all_to_all | solution.py:156
  39.9 1.9 fusion.50
  43.8 1.9 collective-permute-start.5
  48.0 4.2 %collective-permute-done.5 = bf16[2,2,2,8192]{3,2,1,0:T(2,128)(2,1)} collective-permute-done((bf16[2,2,2,8192]{3,2,1,0:T(2,128)(2,1)}, bf16[2,2,2,8192]{3,2,1,0:T(2,128)(2,1)}, u32[]{:S(2)}, u32[]{:S(2)}) %collective-permute-start.5) | collective-permute-done | bytes 131104 | tf_op jit(solution)/shard_map/ppermute | solution.py:14
  53.6 1.4 fusion.28
  55.6 4.0 %collective-permute-start.6 = (bf16[1,4,2,8192]{3,2,1,0:T(2,128)(2,1)S(1)}, bf16[1,4,2,8192]{3,2,1,0:T(2,128)(2,1)S(1)}, u32[]{:S(2)}, u32[]{:S(2)}) collective-permute-start(bf16[1,4,2,8192]{3,2,1,0:T(2,128)(2,1)S(1)} %get-tuple-element.23), channel_id=1, source_target_pairs={{0,8},{2,10},{4,12},{6,14},{8,0},{10,2},{12,4},{14,6},{1,9},{3,11}... | collective-permute-start | bytes 393224 | tf_op jit(solution)/shard_map/ppermute | solution.py:14
  59.7 23.2 %collective-permute-done.1 = bf16[2,2,2,128,512]{4,3,2,1,0:T(8,128)(2,1)S(1)} collective-permute-done((bf16[2,2,2,128,512]{4,3,2,1,0:T(8,128)(2,1)S(1)}, bf16[2,2,2,128,512]{4,3,2,1,0:T(8,128)(2,1)S(1)}, u32[]{:S(2)}, u32[]{:S(2)}) %collective-permute-start.1) | collective-permute-done | bytes 1048608 | tf_op jit(solution)/shard_map/ppermute | solution.py:14
  84.3 1.8 collective-permute-start.2
  87.6 9.3 %fusion.33 = f32[8,2,128,2048]{3,2,1,0:T(8,128)} fusion(bf16[8,2,128,64]{3,2,1,0:T(8,128)(2,1)} %reshape.353, bf16[2048,64]{1,0:T(8,128)(2,1)} %select_n.141), kind=kOutput, calls=%fused_computation.57 | convolution fusion | flops 536870912 | bytes 17301504 | tf_op jit(solution)/shard_map/omshr,opr->omshp/dot_general | solution.py:19
  96.9 35.2 %collective-permute-done.2 = bf16[1,4,2,128,512]{4,3,2,1,0:T(8,128)(2,1)} collective-permute-done((bf16[1,4,2,128,512]{4,3,2,1,0:T(8,128)(2,1)}, bf16[1,4,2,128,512]{4,3,2,1,0:T(8,128)(2,1)}, u32[]{:S(2)}, u32[]{:S(2)}) %collective-permute-start.2) | collective-permute-done | bytes 1048608 | tf_op jit(solution)/shard_map/ppermute | solution.py:14
  132.1 1.5 pad_maximum_fusion.1
  133.6 14.6 %fusion.70 = (f32[8,2,128]{2,1,0:T(2,128)S(1)}, f32[8,2,128,2048]{3,2,1,0:T(8,128)}) fusion(f32[8,2,128,2048]{3,2,1,0:T(8,128)} %fusion.33, bf16[8,2,128,512]{3,2,1,0:T(8,128)(2,1)S(1)} %bitcast.159, bf16[1024,512]{1,0:T(8,128)(2,1)} %collective-permute-done.3, bf16[1024,512]{1,0:T(8,128)(2,1)S(1)} %bitcast.170, pred[]{:T(512)S(6)} %eq.48), kind=kOutput, calls=%fused_computation.143 | convolution fusion | flops 4316985344 | bytes 37756928 | tf_op jit(solution)/shard_map/omshc,opc->omshp/dot_general | solution.py:18
  148.2 8.2 %fusion.1 = f32[8,2,128]{2,1,0:T(2,128)S(1)} fusion(f32[8,2,128,2048]{3,2,1,0:T(8,128)} %get-tuple-element.35, f32[8,2,128]{2,1,0:T(2,128)S(1)} %get-tuple-element.34), kind=kLoop, calls=%fused_computation.8 | loop fusion | flops 8386560 | bytes 16793600 | tf_op jit(solution)/shard_map/reduce_sum | solution.py:25
  156.4 11.4 %divide_convert_fusion.1 = bf16[8,2,128,512]{3,2,1,0:T(8,128)(2,1)S(1)} fusion(f32[8,2,128,2048]{3,2,1,0:T(8,128)} %get-tuple-element.35, f32[8,2,128]{2,1,0:T(2,128)S(1)} %get-tuple-element.34, f32[8,2,128]{2,1,0:T(2,128)S(1)} %fusion.1, bf16[1024,512]{1,0:T(8,128)(2,1)} %collective-permute-done.3, bf16[1024,512]{1,0:T(8,128)(2,1)S(1)} %bitcast.171, ...), kind=kOutput, calls=%fused_computation.14 | convolution fusion | flops 4314890240 | bytes 20987904 | tf_op jit(solution)/shard_map/omshp,opc->omshc/dot_general | solution.py:27
  167.8 1.5 fusion.64
  169.3 1.4 collective-permute-start.11
  171.8 2.0 reshape.361
  173.8 20.2 %collective-permute-done.11 = bf16[4,1,2,128,512]{4,3,2,0,1:T(8,128)(2,1)S(1)} collective-permute-done((bf16[4,1,2,128,512]{4,3,2,0,1:T(8,128)(2,1)}, bf16[4,1,2,128,512]{4,3,2,0,1:T(8,128)(2,1)S(1)}, u32[]{:S(2)}, u32[]{:S(2)}) %collective-permute-start.11) | collective-permute-done | bytes 1048608 | tf_op jit(solution)/shard_map/ppermute | solution.py:14
  194.9 2.9 fusion.27
  198.8 3.7 %convolution_convert_fusion = bf16[32,7168]{1,0:T(8,128)(2,1)} fusion(bf16[1,128,7168]{2,1,0:T(8,128)(2,1)} %param.27, bf16[32,7168]{1,0:T(8,128)(2,1)} %reshape.361, bf16[1,7168,128]{2,1,0:T(8,128)(2,1)} %param.26, f32[32,128]{1,0:T(8,128)S(1)} %fusion.13), kind=kOutput, calls=%fused_computation.11 | convolution fusion | flops 117694464 | bytes 4603904 | tf_op jit(solution)/shard_map/dot_general | solution.py:162
  202.6 2.0 reshape.362
  204.5 4.8 %all-to-all-start.1 = ((bf16[16,2,7168]{2,1,0:T(2,128)(2,1)}), bf16[16,2,7168]{2,1,0:T(2,128)(2,1)}, u32[]{:S(2)}, u32[]{:S(2)}) async-start(bf16[16,2,7168]{2,1,0:T(2,128)(2,1)} %reshape.362), calls=%async_computation.1 | async-start | bytes 917504 | tf_op jit(solution)/shard_map/all_to_all | solution.py:161
  209.4 1.9 collective-permute-start.8
  211.3 2.4 collective-permute-done.8
  213.7 1.5 collective-permute-start.9
  215.2 11.9 %collective-permute-done.12 = bf16[2,2,2,128,512]{4,3,2,0,1:T(8,128)(2,1)} collective-permute-done((bf16[2,2,2,128,512]{4,3,2,0,1:T(8,128)(2,1)}, bf16[2,2,2,128,512]{4,3,2,0,1:T(8,128)(2,1)}, u32[]{:S(2)}, u32[]{:S(2)}) %collective-permute-start.12) | collective-permute-done | bytes 1048608 | tf_op jit(solution)/shard_map/ppermute | solution.py:14
  227.1 1.4 pad_maximum_fusion.2
  229.7 2.3 collective-permute-start.13
  232.0 1.5 convert_reduce_fusion
  233.6 3.3 %gather_fusion.2 = f32[128,7168]{1,0:T(8,128)} fusion(f32[4,7168]{1,0:T(4,128)S(1)} %reshape.363, s32[1024]{0:T(1024)S(1)} %pad_clamp_fusion), kind=kCustom, calls=%fused_computation.4 | custom fusion | bytes 7340544 | tf_op jit(solution)/shard_map/jit(_take)/gather | solution.py:175
  237.6 3.3 %fusion.6 = bf16[16,7168]{1,0:T(8,128)(2,1)S(1)} fusion(f32[128,7168]{1,0:T(8,128)} %gather_fusion.2, f32[16,8]{1,0:T(8,128)S(1)} %broadcast_select_fusion.3, pred[16,8]{1,0:T(8,128)(4,1)S(1)} %copy-done.13), kind=kLoop, calls=%fused_computation.17 | loop fusion | flops 2637824 | bytes 3900032 | tf_op jit(solution)/shard_map/reduce_sum | solution.py:177
  241.7 33.4 %collective-permute-done.10 = f32[1,4,2,128]{3,2,1,0:T(2,128)S(1)} collective-permute-done((f32[1,4,2,128]{3,2,1,0:T(2,128)S(1)}, f32[1,4,2,128]{3,2,1,0:T(2,128)S(1)}, u32[]{:S(2)}, u32[]{:S(2)}) %collective-permute-start.10) | collective-permute-done | bytes 4128 | tf_op jit(solution)/shard_map/ppermute | solution.py:14
  275.7 2.7 pad_maximum_fusion.3
  278.5 3.6 %gather_fusion.4 = bf16[8,2,128,512]{3,2,1,0:T(8,128)(2,1)} fusion(bf16[8,2,128,512]{3,2,1,0:T(8,128)(2,1)} %bitcast.163, s32[1024]{0:T(1024)S(1)} %pad_clamp_fusion.1), kind=kCustom, calls=%fused_computation.1.clone | custom fusion | bytes 4194336 | tf_op jit(solution)/shard_map/jit(_take)/gather | solution.py:105
  282.1 5.3 %divide_convert_fusion = bf16[8,2,128,512]{3,2,1,0:T(8,128)(2,1)} fusion(bf16[8,2,128,512]{3,2,1,0:T(8,128)(2,1)} %gather_fusion.4, f32[8,2,128]{2,1,0:T(2,128)S(1)} %get-tuple-element.5, f32[8,2,128]{2,1,0:T(2,128)S(1)} %get-tuple-element.6, f32[8,2,128]{2,1,0:T(2,128)S(1)} %get-tuple-element.7, pred[8]{0:T(512)(128)(4,1)S(1)} %copy-done.17, ...), kind=kOutput, calls=%fused_computation.13 | convolution fusion | flops 32514048 | bytes 4259852 | tf_op jit(solution)/shard_map/rshj,rjc->rshc/dot_general | solution.py:118
  (109 shorter events, 26.0 us)
Async XLA Ops:
  0.6 1.8 copy-start
  1.9 0.5 copy-start.18
  6.3 4.3 %copy-start.5 = (bf16[8,2,8192]{2,1,0:T(2,128)(2,1)S(1)}, bf16[8,2,8192]{2,1,0:T(2,128)(2,1)}, u32[]{:S(2)}) copy-start(bf16[8,2,8192]{2,1,0:T(2,128)(2,1)} %param.18) | copy-start | bytes 786436
  6.4 8.6 %copy-start.7 = (s32[8,2,8]{2,1,0:T(2,128)S(1)}, s32[8,2,8]{2,1,0:T(2,128)}, u32[]{:S(2)}) copy-start(s32[8,2,8]{2,1,0:T(2,128)} %param.23) | copy-start | bytes 1540
  7.5 46.0 %collective-permute-start = (bf16[4,1,2,128,512]{4,3,2,0,1:T(8,128)(2,1)}, bf16[4,1,2,128,512]{4,3,2,0,1:T(8,128)(2,1)}, u32[]{:S(2)}, u32[]{:S(2)}) collective-permute-start(bf16[4,1,2,128,512]{4,3,2,0,1:T(8,128)(2,1)} %get-tuple-element.21), channel_id=1, source_target_pairs={{0,2},{2,0},{4,6},{6,4},{8,10},{10,8},{12,14},{14,12},{1,3},{3,1},... | collective-permute-start | bytes 3145736 | tf_op jit(solution)/shard_map/ppermute | solution.py:14
  14.5 27.3 %collective-permute-start.4 = (bf16[4,1,2,8192]{3,2,0,1:T(2,128)(2,1)}, bf16[4,1,2,8192]{3,2,0,1:T(2,128)(2,1)}, u32[]{:S(2)}, u32[]{:S(2)}) collective-permute-start(bf16[4,1,2,8192]{3,2,0,1:T(2,128)(2,1)} %get-tuple-element.27), channel_id=1, source_target_pairs={{0,2},{2,0},{4,6},{6,4},{8,10},{10,8},{12,14},{14,12},{1,3},{3,1},... | collective-permute-start | bytes 393224 | tf_op jit(solution)/shard_map/ppermute | solution.py:14
  14.5 31.3 %collective-permute-start.7 = (bf16[128,512]{1,0:T(8,128)(2,1)}, bf16[128,512]{1,0:T(8,128)(2,1)}, u32[]{:S(2)}, u32[]{:S(2)}) collective-permute-start(bf16[128,512]{1,0:T(8,128)(2,1)} %bitcast.179), channel_id=1, source_target_pairs={{0,1},{1,0},{2,3},{3,2},{4,5},{5,4},{6,7},{7,6},{8,9},{9,8},{10,11... | collective-permute-start | bytes 393224 | tf_op jit(solution)/shard_map/ppermute | solution.py:14
  14.5 119.1 %collective-permute-start.3 = (bf16[1024,512]{1,0:T(8,128)(2,1)}, bf16[1024,512]{1,0:T(8,128)(2,1)}, u32[]{:S(2)}, u32[]{:S(2)}) collective-permute-start(bf16[1024,512]{1,0:T(8,128)(2,1)} %bitcast.169), channel_id=1, source_target_pairs={{0,1},{1,0},{2,3},{3,2},{4,5},{5,4},{6,7},{7,6},{8,9},{9,8},{10,11... | collective-permute-start | bytes 3145736 | tf_op jit(solution)/shard_map/ppermute | solution.py:14
  24.1 15.8 %copy-start.16 = (bf16[8,2,64]{2,1,0:T(2,128)(2,1)S(1)}, bf16[8,2,64]{2,1,0:T(2,128)(2,1)}, u32[]{:S(2)}) copy-start(bf16[8,2,64]{2,1,0:T(2,128)(2,1)} %param.20) | copy-start | bytes 6148
  27.2 18.5 %copy-start.19 = (s32[8]{0:T(128)S(1)}, s32[8]{0:T(128)}, u32[]{:S(2)}) copy-start(s32[8]{0:T(128)} %copy-done.18) | copy-start | bytes 100
  32.2 139.6 %all-to-all-start = ((bf16[16,2,7168]{2,1,0:T(2,128)(2,1)}), bf16[16,2,7168]{2,1,0:T(2,128)(2,1)}, u32[]{:S(2)}, u32[]{:S(2)}) async-start(bf16[16,2,7168]{2,1,0:T(2,128)(2,1)} %bitcast.168), calls=%async_computation | async-start | bytes 917504 | tf_op jit(solution)/shard_map/all_to_all | solution.py:156
  43.8 8.5 %collective-permute-start.5 = (bf16[2,2,2,8192]{3,2,1,0:T(2,128)(2,1)}, bf16[2,2,2,8192]{3,2,1,0:T(2,128)(2,1)}, u32[]{:S(2)}, u32[]{:S(2)}) collective-permute-start(bf16[2,2,2,8192]{3,2,1,0:T(2,128)(2,1)} %bitcast.154), channel_id=1, source_target_pairs={{0,4},{2,6},{4,0},{6,2},{8,12},{10,14},{12,8},{14,10},{1,5},{3,7},... | collective-permute-start | bytes 393224 | tf_op jit(solution)/shard_map/ppermute | solution.py:14
  55.0 27.9 %collective-permute-start.1 = (bf16[2,2,2,128,512]{4,3,2,1,0:T(8,128)(2,1)S(1)}, bf16[2,2,2,128,512]{4,3,2,1,0:T(8,128)(2,1)S(1)}, u32[]{:S(2)}, u32[]{:S(2)}) collective-permute-start(bf16[2,2,2,128,512]{4,3,2,1,0:T(8,128)(2,1)S(1)} %bitcast.173), channel_id=1, source_target_pairs={{0,4},{2,6},{4,0},{6,2},{8,12},{10,14},{12,8},{14,10},{1,5},{3,7},... | collective-permute-start | bytes 3145736 | tf_op jit(solution)/shard_map/ppermute | solution.py:14
  55.6 30.5 %collective-permute-start.6 = (bf16[1,4,2,8192]{3,2,1,0:T(2,128)(2,1)S(1)}, bf16[1,4,2,8192]{3,2,1,0:T(2,128)(2,1)S(1)}, u32[]{:S(2)}, u32[]{:S(2)}) collective-permute-start(bf16[1,4,2,8192]{3,2,1,0:T(2,128)(2,1)S(1)} %get-tuple-element.23), channel_id=1, source_target_pairs={{0,8},{2,10},{4,12},{6,14},{8,0},{10,2},{12,4},{14,6},{1,9},{3,11}... | collective-permute-start | bytes 393224 | tf_op jit(solution)/shard_map/ppermute | solution.py:14
  84.3 47.8 %collective-permute-start.2 = (bf16[1,4,2,128,512]{4,3,2,1,0:T(8,128)(2,1)}, bf16[1,4,2,128,512]{4,3,2,1,0:T(8,128)(2,1)}, u32[]{:S(2)}, u32[]{:S(2)}) collective-permute-start(bf16[1,4,2,128,512]{4,3,2,1,0:T(8,128)(2,1)} %get-tuple-element.17), channel_id=1, source_target_pairs={{0,8},{2,10},{4,12},{6,14},{8,0},{10,2},{12,4},{14,6},{1,9},{3,11}... | collective-permute-start | bytes 3145736 | tf_op jit(solution)/shard_map/ppermute | solution.py:14
  132.1 1.5 copy-start.3
  148.2 8.2 %copy-start.4 = (bf16[1,1024,512]{2,1,0:T(8,128)(2,1)S(1)}, bf16[1,1024,512]{2,1,0:T(8,128)(2,1)}, u32[]{:S(2)}) copy-start(bf16[1,1024,512]{2,1,0:T(8,128)(2,1)} %param.15) | copy-start | bytes 3145732
  167.8 3.0 %copy-start.9 = (pred[8,2,8]{2,1,0:T(4,128)(4,1)S(1)}, pred[8,2,8]{2,1,0:T(4,128)(4,1)}, u32[]{:S(2)}) copy-start(pred[8,2,8]{2,1,0:T(4,128)(4,1)} %broadcast_compare_fusion) | copy-start | bytes 388
  167.8 3.1 %copy-start.8 = (f32[8,2,128,2]{2,3,1,0:T(2,128)S(1)}, f32[8,2,128,2]{2,3,1,0:T(2,128)}, u32[]{:S(2)}) copy-start(f32[8,2,128,2]{2,3,1,0:T(2,128)} %fusion.50) | copy-start | bytes 49156
  167.8 3.1 %copy-start.11 = (bf16[8,2,512]{2,1,0:T(2,128)(2,1)S(1)}, bf16[8,2,512]{2,1,0:T(2,128)(2,1)}, u32[]{:S(2)}) copy-start(bf16[8,2,512]{2,1,0:T(2,128)(2,1)} %param.19) | copy-start | bytes 49156
  169.3 2.4 copy-start.15
  169.3 2.4 copy-start.10
  169.3 2.4 copy-start.14
  169.3 24.6 %collective-permute-start.11 = (bf16[4,1,2,128,512]{4,3,2,0,1:T(8,128)(2,1)}, bf16[4,1,2,128,512]{4,3,2,0,1:T(8,128)(2,1)S(1)}, u32[]{:S(2)}, u32[]{:S(2)}) collective-permute-start(bf16[4,1,2,128,512]{4,3,2,0,1:T(8,128)(2,1)} %get-tuple-element.15), channel_id=1, source_target_pairs={{0,2},{2,0},{4,6},{6,4},{8,10},{10,8},{12,14},{14,12},{1,3},{3,1},... | collective-permute-start | bytes 3145736 | tf_op jit(solution)/shard_map/ppermute | solution.py:14
  194.0 1.0 copy-start.6
  194.9 3.5 %copy-start.1 = (bf16[32,7168]{1,0:T(8,128)(2,1)S(1)}, bf16[32,7168]{1,0:T(8,128)(2,1)}, u32[]{:S(2)}) copy-start(bf16[32,7168]{1,0:T(8,128)(2,1)} %reshape.361) | copy-start | bytes 1376260
  194.9 3.5 %copy-start.2 = (bf16[1,7168,128]{2,1,0:T(8,128)(2,1)S(1)}, bf16[1,7168,128]{2,1,0:T(8,128)(2,1)}, u32[]{:S(2)}) copy-start(bf16[1,7168,128]{2,1,0:T(8,128)(2,1)} %param.25) | copy-start | bytes 5505028
  197.8 29.3 %collective-permute-start.12 = (bf16[2,2,2,128,512]{4,3,2,0,1:T(8,128)(2,1)}, bf16[2,2,2,128,512]{4,3,2,0,1:T(8,128)(2,1)}, u32[]{:S(2)}, u32[]{:S(2)}) collective-permute-start(bf16[2,2,2,128,512]{4,3,2,0,1:T(8,128)(2,1)} %get-tuple-element.13), channel_id=1, source_target_pairs={{0,4},{2,6},{4,0},{6,2},{8,12},{10,14},{12,8},{14,10},{1,5},{3,7},... | collective-permute-start | bytes 3145736 | tf_op jit(solution)/shard_map/ppermute | solution.py:14
  204.5 27.5 %all-to-all-start.1 = ((bf16[16,2,7168]{2,1,0:T(2,128)(2,1)}), bf16[16,2,7168]{2,1,0:T(2,128)(2,1)}, u32[]{:S(2)}, u32[]{:S(2)}) async-start(bf16[16,2,7168]{2,1,0:T(2,128)(2,1)} %reshape.362), calls=%async_computation.1 | async-start | bytes 917504 | tf_op jit(solution)/shard_map/all_to_all | solution.py:161
  209.4 4.3 %collective-permute-start.8 = (f32[4,1,2,128]{3,2,0,1:T(2,128)S(1)}, f32[4,1,2,128]{3,2,0,1:T(2,128)S(1)}, u32[]{:S(2)}, u32[]{:S(2)}) collective-permute-start(f32[4,1,2,128]{3,2,0,1:T(2,128)S(1)} %get-tuple-element.33), channel_id=1, source_target_pairs={{0,2},{2,0},{4,6},{6,4},{8,10},{10,8},{12,14},{14,12},{1,3},{3,1},... | collective-permute-start | bytes 12296 | tf_op jit(solution)/shard_map/ppermute | solution.py:14
  213.7 23.1 %collective-permute-start.9 = (f32[2,2,2,128]{3,2,0,1:T(2,128)S(1)}, f32[2,2,2,128]{3,2,0,1:T(2,128)S(1)}, u32[]{:S(2)}, u32[]{:S(2)}) collective-permute-start(f32[2,2,2,128]{3,2,0,1:T(2,128)S(1)} %get-tuple-element.31), channel_id=1, source_target_pairs={{0,4},{2,6},{4,0},{6,2},{8,12},{10,14},{12,8},{14,10},{1,5},{3,7},... | collective-permute-start | bytes 12296 | tf_op jit(solution)/shard_map/ppermute | solution.py:14
  229.7 46.0 %collective-permute-start.13 = (bf16[1,4,2,128,512]{4,3,2,1,0:T(8,128)(2,1)}, bf16[1,4,2,128,512]{4,3,2,1,0:T(8,128)(2,1)}, u32[]{:S(2)}, u32[]{:S(2)}) collective-permute-start(bf16[1,4,2,128,512]{4,3,2,1,0:T(8,128)(2,1)} %get-tuple-element.11), channel_id=1, source_target_pairs={{0,8},{2,10},{4,12},{6,14},{8,0},{10,2},{12,4},{14,6},{1,9},{3,11}... | collective-permute-start | bytes 3145736 | tf_op jit(solution)/shard_map/ppermute | solution.py:14
  233.6 4.0 %copy-start.13 = (pred[16,8]{1,0:T(8,128)(4,1)S(1)}, pred[16,8]{1,0:T(8,128)(4,1)}, u32[]{:S(2)}) copy-start(pred[16,8]{1,0:T(8,128)(4,1)} %get-tuple-element.3) | copy-start | bytes 388
  236.9 38.2 %collective-permute-start.10 = (f32[1,4,2,128]{3,2,1,0:T(2,128)S(1)}, f32[1,4,2,128]{3,2,1,0:T(2,128)S(1)}, u32[]{:S(2)}, u32[]{:S(2)}) collective-permute-start(f32[1,4,2,128]{3,2,1,0:T(2,128)S(1)} %get-tuple-element.29), channel_id=1, source_target_pairs={{0,8},{2,10},{4,12},{6,14},{8,0},{10,2},{12,4},{14,6},{1,9},{3,11}... | collective-permute-start | bytes 12296 | tf_op jit(solution)/shard_map/ppermute | solution.py:14
  237.6 38.0 %copy-start.17 = (pred[8]{0:T(512)(128)(4,1)S(1)}, pred[8]{0:T(512)(128)(4,1)}, u32[]{:S(2)}) copy-start(pred[8]{0:T(512)(128)(4,1)} %get-tuple-element.8) | copy-start | bytes 28
  278.5 3.6 %copy-start.12 = (bf16[8,2,512]{2,1,0:T(2,128)(2,1)S(1)}, bf16[8,2,512]{2,1,0:T(2,128)(2,1)}, u32[]{:S(2)}) copy-start(bf16[8,2,512]{2,1,0:T(2,128)(2,1)} %param.19) | copy-start | bytes 49156
where the time goes:
time: 289 us; the launch traced here: 287 us
  waiting for transfers between devices  131 us (45%)
  matrix products  48.9 us (17%)
  other arithmetic  39 us (13%)
  local copies, waits for them, and re-layouts  36.6 us (13%)
  starting transfers between devices  31.2 us (11%)
    ppermute x14, waiting for transfers between devices, swapped(): lax.ppermute(x, axis, [(i, i ^ 1 << bit) for i in range(lax.axis_size(axi...  131 us
    ppermute x14, starting transfers between devices, swapped(): lax.ppermute(x, axis, [(i, i ^ 1 << bit) for i in range(lax.axis_size(axi...  20 us
    dot_general x1, matrix products, partial_softmax(): jnp.einsum('omshc,opc->omshp', query_lat, keys_lat, preferred_element_typ...  14.6 us
    dot_general x1, matrix products, partial_softmax(): jnp.einsum('omshp,opc->omshc', weights, keys_lat, preferred_element_type=...  11.4 us
    another operation x10, other arithmetic, join_half(): jnp.stack([staying, arrived], axis=1).reshape((-1,) + staying.shape[2:])  10.2 us
    dot_general x1, matrix products, partial_softmax(): jnp.einsum('omshr,opr->omshp', query_rope, keys_rope, preferred_element_t...  9.26 us
    reduce_sum x1, other arithmetic, partial_softmax(): totals = jnp.sum(exponent, axis=-1)  8.23 us
    all_to_all x1, starting transfers between devices, on_device(): lax.all_to_all(copies, ('branch', 'expert'), split_axis=0, concat_axis=0,...  6.5 us
  transfers between devices with their start and end apart: 16, of which 7 were waited for; matrix products, arithmetic and copies ran while one was open for 36% of the time, Pallas kernels for 0%

commit v1 on v0

v1 whole, which is shorter than its diff:
```python
import functools

import jax
import jax.numpy as jnp
from jax import lax
from jax.experimental import pallas as pl
from jax.experimental.pallas import tpu as pltpu
from jax.sharding import PartitionSpec as P

SHARDS = 8
CAP = 2
HALF = 4
CHUNKS = 4

softmax_scale = 192.0 ** (-0.5)


def flipped(r, x, bits):
    out = r - r % (1 << bits)
    for j in range(bits):
        out = out + (((r // (1 << j)) + (x // (1 << j))) % 2) * (1 << j)
    return out


def attend_kernel(
    ordering_ref,
    target_ref,
    q_ref,
    rope_ref,
    new_ref,
    keys_ref,
    krope_ref,
    out_ref,
    q_send,
    rope_send,
    new_send,
    q_in,
    rope_in,
    new_in,
    keys,
    kpack,
    kdup,
    result,
    answers,
    sib_send,
    sib_recv,
    part_send,
    part_recv,
    fwd_send,
    fwd_recv,
    query_send,
    query_recv,
    ans_send,
    ans_recv,
):
    branch = lax.axis_index("branch")
    core = lax.axis_index("expert")
    tok = q_ref.shape[0]
    rows = q_ref.shape[1]
    half_len = keys_ref.shape[0]
    packed_len = krope_ref.shape[0]
    heads = rope_ref.shape[1]
    lanes = rope_ref.shape[2]
    step_rows = half_len // CHUNKS
    pack_rows = packed_len // CHUNKS

    def place(b, c):
        return {"branch": b, "expert": c}

    sibling = place(branch, 1 - core)
    partner = place(flipped(branch, HALF, 3), core)

    def peer(x):
        return place(flipped(branch, x % HALF, 3), core)

    barrier = pltpu.get_barrier_semaphore()
    for other in [sibling, partner] + [peer(j) for j in range(1, HALF)]:
        pl.semaphore_signal(
            barrier, inc=1, device_id=other, device_id_type=pl.DeviceIdType.MESH
        )
    pl.semaphore_wait(barrier, 2 + HALF - 1)

    def remote(src, dst, send, recv, where):
        return pltpu.make_async_remote_copy(
            src_ref=src,
            dst_ref=dst,
            send_sem=send,
            recv_sem=recv,
            device_id=where,
            device_id_type=pl.DeviceIdType.MESH,
        )

    def sib_copies():
        return [
            remote(keys_ref, keys.at[0], sib_send.at[0], sib_recv.at[0], sibling),
            remote(krope_ref, kpack.at[0], sib_send.at[1], sib_recv.at[1], sibling),
        ]

    def part_copies(c):
        big = pl.ds(c * step_rows, step_rows)
        small = pl.ds(c * pack_rows, pack_rows)
        return [
            remote(
                keys_ref.at[big], keys.at[1, big], part_send.at[0, c], part_recv.at[0, c], partner
            ),
            remote(
                krope_ref.at[small],
                kpack.at[1, small],
                part_send.at[1, c],
                part_recv.at[1, c],
                partner,
            ),
        ]

    def fwd_copies(c):
        big = pl.ds(c * step_rows, step_rows)
        small = pl.ds(c * pack_rows, pack_rows)
        return [
            remote(
                keys.at[1, big], keys.at[2, big], fwd_send.at[0, c], fwd_recv.at[0, c], sibling
            ),
            remote(
                kpack.at[1, small], kpack.at[2, small], fwd_send.at[1, c], fwd_recv.at[1, c], sibling
            ),
        ]

    def query_copies(x):
        where = peer(x)
        return [
            remote(q_send.at[x], q_in.at[x], query_send.at[0, x], query_recv.at[0, x], where),
            remote(rope_send.at[x], rope_in.at[x], query_send.at[1, x], query_recv.at[1, x], where),
            remote(new_send.at[x], new_in.at[x], query_send.at[2, x], query_recv.at[2, x], where),
        ]

    def answer_copy(x):
        return remote(result.at[x], answers.at[x], ans_send.at[x], ans_recv.at[x], peer(x))

    def gather(x, to_q, to_rope, to_new):
        at = ordering_ref[x]
        to_q[x] = q_ref[at]
        to_rope[x] = rope_ref[at]
        to_new[x] = new_ref[at]

    for copy in sib_copies():
        copy.start()
    order = [2, 3, 6, 7]
    for c in range(CHUNKS):
        for copy in part_copies(c):
            copy.start()
        x = order[c]
        gather(x, q_send, rope_send, new_send)
        for copy in query_copies(x):
            copy.start()
        if c % 2 == 0:
            y = (1, 5)[c // 2]
            gather(y, q_send, rope_send, new_send)
            for copy in query_copies(y):
                copy.start()
    for x in (0, HALF):
        gather(x, q_in, rope_in, new_in)

    lane = lax.broadcasted_iota(jnp.int32, (packed_len, lanes), 1)
    low = lane < lanes // 2

    def spread(packed, slot):
        values = packed.astype(jnp.float32)
        turned = pltpu.roll(values, lanes // 2, 1)
        kdup[slot, pl.ds(0, packed_len)] = jnp.where(low, values, turned).astype(jnp.bfloat16)
        kdup[slot, pl.ds(packed_len, packed_len)] = jnp.where(low, turned, values).astype(
            jnp.bfloat16
        )

    nt = (((1,), (1,)), ((), ()))
    nn = (((1,), (0,)), ((), ()))
    head_low = lax.broadcasted_iota(jnp.int32, (heads, lanes), 1) < lanes // 2
    second = lax.broadcasted_iota(jnp.int32, (rows, 1), 0) >= heads

    def attend(x, first_keys, first_rope, other_keys, other_rope):
        q = q_in[x]
        packed = rope_in[x].astype(jnp.float32)
        qr = jnp.concatenate(
            [jnp.where(head_low, packed, 0.0), jnp.where(head_low, 0.0, packed)], axis=0
        ).astype(jnp.bfloat16)
        fresh = new_in[x]
        lat = q.shape[1]

        def score(k, kr):
            return lax.dot_general(
                q, k, nt, preferred_element_type=jnp.float32
            ) + lax.dot_general(qr, kr, nt, preferred_element_type=jnp.float32)

        own = score(fresh[:, :lat], fresh[:, lat:])
        own0 = own[:, 0:1]
        own1 = jnp.where(second, own[:, 1:2], -1e30)
        s0 = score(first_keys[...], first_rope[...])
        s1 = score(other_keys[...], other_rope[...])
        top = jnp.maximum(jnp.max(s0, axis=1, keepdims=True), jnp.max(s1, axis=1, keepdims=True))
        top = jnp.maximum(top, jnp.maximum(own0, own1))
        p0 = jnp.exp((s0 - top) * softmax_scale)
        p1 = jnp.exp((s1 - top) * softmax_scale)
        w0 = jnp.exp((own0 - top) * softmax_scale)
        w1 = jnp.where(second, jnp.exp((own1 - top) * softmax_scale), 0.0)
        total = jnp.sum(p0, axis=1, keepdims=True) + jnp.sum(p1, axis=1, keepdims=True) + w0 + w1
        summed = lax.dot_general(
            p0.astype(jnp.bfloat16), first_keys[...], nn, preferred_element_type=jnp.float32
        ) + lax.dot_general(
            p1.astype(jnp.bfloat16), other_keys[...], nn, preferred_element_type=jnp.float32
        )
        entries = fresh[:, :lat].astype(jnp.float32)
        summed = summed + w0 * entries[0:1] + w1 * entries[1:2]
        return (summed / total).astype(jnp.bfloat16)

    def run(start, *cache):
        answers[start] = attend(start, *cache)

        def body(x, carry):
            for copy in query_copies(x):
                copy.wait_recv()
            result[x] = attend(x, *cache)
            answer_copy(x).start()
            return carry

        lax.fori_loop(start + 1, start + HALF, body, 0)

    spread(krope_ref[...], 0)
    for copy in sib_copies():
        copy.wait_recv()
    spread(kpack[0], 1)
    run(0, keys_ref, kdup.at[0], keys.at[0], kdup.at[1])

    for c in range(CHUNKS):
        for copy in part_copies(c):
            copy.wait_recv()
        for copy in fwd_copies(c):
            copy.start()
    spread(kpack[1], 2)
    for c in range(CHUNKS):
        for copy in fwd_copies(c):
            copy.wait_recv()
    spread(kpack[2], 3)
    run(HALF, keys.at[1], kdup.at[2], keys.at[2], kdup.at[3])

    for x in range(tok):
        if x % HALF:
            answer_copy(x).wait_recv()
    for t in range(tok):
        out_ref[t] = answers[target_ref[t]]
    for copy in sib_copies():
        copy.wait_send()
    for c in range(CHUNKS):
        for copy in part_copies(c) + fwd_copies(c):
            copy.wait_send()
    for x in range(tok):
        if x % HALF:
            for copy in query_copies(x):
                copy.wait_send()
            answer_copy(x).wait_send()


def attention(ordering, target, q, rope, new, keys, krope):
    tok, rows, lat = q.shape
    heads, lanes = rope.shape[1:]
    half_len = keys.shape[0]
    packed_len = krope.shape[0]
    bf = jnp.bfloat16
    vmem = pl.BlockSpec(memory_space=pltpu.VMEM)
    smem = pl.BlockSpec(memory_space=pltpu.SMEM)
    dma = pltpu.SemaphoreType.DMA
    return pl.pallas_call(
        attend_kernel,
        out_shape=jax.ShapeDtypeStruct(q.shape, bf),
        in_specs=[smem, smem] + [vmem] * 5,
        out_specs=vmem,
        scratch_shapes=[
            pltpu.VMEM(q.shape, bf),
            pltpu.VMEM(rope.shape, bf),
            pltpu.VMEM(new.shape, bf),
            pltpu.VMEM(q.shape, bf),
            pltpu.VMEM(rope.shape, bf),
            pltpu.VMEM(new.shape, bf),
            pltpu.VMEM((3, half_len, lat), bf),
            pltpu.VMEM((3, packed_len, lanes), bf),
            pltpu.VMEM((4, half_len, lanes), bf),
            pltpu.VMEM(q.shape, bf),
            pltpu.VMEM(q.shape, bf),
            dma((2,)),
            dma((2,)),
            dma((2, CHUNKS)),
            dma((2, CHUNKS)),
            dma((2, CHUNKS)),
            dma((2, CHUNKS)),
            dma((3, tok)),
            dma((3, tok)),
            dma((tok,)),
            dma((tok,)),
        ],
        compiler_params=pltpu.CompilerParams(
            collective_id=0, has_side_effects=True, vmem_limit_bytes=56 * 1024 * 1024
        ),
    )(ordering, target, q, rope, new, keys, krope)


def on_device(
    latent_cache,
    rope_cache,
    q_latent,
    q_rope,
    new_latent,
    new_rope,
    branch_slot,
    moe_input,
    routes,
    route_gate,
    w_gate,
    w_up,
    w_down,
):
    tok_rows, step_count, head_count, lat = q_latent.shape
    rope_width = new_rope.shape[-1]

    model_width = moe_input.shape[-1]
    tok_total = tok_rows * step_count
    expert_count = lax.axis_size("branch") * lax.axis_size("expert") // SHARDS
    slots = expert_count * CAP
    flat = routes.reshape(tok_total, -1)
    chosen = (flat[:, :, None] == jnp.arange(expert_count, dtype=jnp.int32)).astype(jnp.float32)
    gate = jnp.sum(chosen * route_gate.reshape(tok_total, -1, 1), axis=1)
    hit = jnp.sum(chosen, axis=1)
    earlier = (jnp.arange(tok_total)[:, None] > jnp.arange(tok_total)[None, :]).astype(jnp.float32)
    position = jnp.sum(earlier[:, :, None] * hit[None], axis=1)
    placing = hit[:, :, None] * (position[:, :, None] == jnp.arange(CAP, dtype=jnp.float32))
    weights = (placing * gate[:, :, None]).reshape(tok_total, slots)
    placing = placing.reshape(tok_total, slots).astype(jnp.bfloat16)
    tokens_flat = moe_input.reshape(tok_total, model_width)
    outgoing = lax.dot_general(
        placing, tokens_flat, (((0,), (0,)), ((), ())), preferred_element_type=jnp.float32
    ).astype(jnp.bfloat16)
    outgoing = outgoing.reshape(expert_count, 1, CAP, model_width)
    copies = jnp.broadcast_to(outgoing, (expert_count, SHARDS, CAP, model_width))
    copies = copies.reshape(expert_count * SHARDS, CAP, model_width)
    arrived = lax.all_to_all(copies, ("branch", "expert"), split_axis=0, concat_axis=0, tiled=True)
    flattened = arrived.reshape(-1, model_width)
    gate_value = jnp.dot(flattened, w_gate[0], preferred_element_type=jnp.float32)
    lifted = jnp.dot(flattened, w_up[0], preferred_element_type=jnp.float32)
    hidden = (jax.nn.silu(gate_value) * lifted).astype(jnp.bfloat16)
    returned = lax.all_to_all(
        jnp.dot(hidden, w_down[0], preferred_element_type=jnp.float32)
        .astype(jnp.bfloat16)
        .reshape(arrived.shape),
        ("branch", "expert"),
        split_axis=0,
        concat_axis=0,
        tiled=True,
    )
    expert_sums = jnp.sum(
        returned.reshape(expert_count, SHARDS, CAP, model_width).astype(jnp.float32), axis=1
    ).reshape(slots, model_width)
    combined = jnp.sum(weights[:, :, None] * expert_sums[None], axis=1)
    moe_out = combined.astype(jnp.bfloat16).reshape(tok_rows, step_count, model_width)

    counting = jnp.arange(tok_rows, dtype=jnp.int32)
    own_index = lax.axis_index("branch") % tok_rows
    target = jnp.bitwise_xor(own_index, branch_slot)
    chooser = (target[None, :] == counting[:, None]).astype(jnp.int32)
    ordering = jnp.sum(chooser * counting[None, :], axis=1)
    rope = q_rope.reshape(tok_rows, step_count, head_count, rope_width)
    rope = rope.transpose(0, 2, 1, 3).reshape(tok_rows, head_count, step_count * rope_width)
    new = jnp.concatenate([new_latent, new_rope, new_rope], axis=-1)
    new = jnp.pad(new, ((0, 0), (0, 8 - step_count), (0, 0)))
    krope = rope_cache[0].reshape(2, -1, rope_width)
    krope = jnp.concatenate([krope[0], krope[1]], axis=-1)
    attended = attention(
        ordering,
        target,
        q_latent.reshape(tok_rows, step_count * head_count, lat),
        rope,
        new,
        latent_cache[0],
        krope,
    )
    attended = attended.reshape(q_latent.shape)
    return (attended, moe_out)


def solution(mesh):
    return jax.shard_map(
        on_device,
        mesh=mesh,
        in_specs=(
            P(("group", "branch"), "expert", None),
            P(("group", "branch"), "expert", None),
            P(("group", "branch", "expert"), None, None, None),
            P(("group", "branch", "expert"), None, None),
            P(("group", "branch", "expert"), None, None),
            P(("group", "branch", "expert"), None, None),
            P(("group", "branch", "expert")),
            P(("group", "branch", "expert"), None, None),
            P(("group", "branch", "expert"), None, None),
            P(("group", "branch", "expert"), None, None),
            P(("branch", "expert"), None, None),
            P(("branch", "expert"), None, None),
            P(("branch", "expert"), None, None),
        ),
        out_specs=(
            P(("group", "branch", "expert"), None, None, None),
            P(("group", "branch", "expert"), None, None),
        ),
        check_vma=False,
    )
```

time: 289 us -> 129 us (0.45)
  waiting for transfers between devices: 131 us -> 0.01 us
  Pallas kernels: 0 us -> 85.6 us
  matrix products: 48.9 us -> 4.31 us
  other arithmetic: 39 us -> 2.87 us
  starting transfers between devices: 31.2 us -> 3.8 us
  local copies, waits for them, and re-layouts: 36.6 us -> 10.2 us
  blocking collectives: 0 us -> 20.4 us
    ppermute x14 -> x0, waiting for transfers between devices: 131 us -> none  [swapped(): lax.ppermute(x, axis, [(i, i ^ 1 << bit) for i in range(lax.axis_size(axi...]
    pallas_call x0 -> x1, Pallas kernels: none -> 85.6 us  [attention(): pl.pallas_call(attend_kernel, out_shape=jax.ShapeDtypeStruct(q.shape, bf)...]
    dot_general x7 -> x1, matrix products: 44.8 us -> 0.16 us  [on_device(): lax.dot_general(placing, tokens_flat, (((0,), (0,)), ((), ())), preferred...]
    all_to_all x0 -> x1, blocking collectives: none -> 20.4 us  [on_device(): lax.all_to_all(copies, ('branch', 'expert'), split_axis=0, concat_axis=0,...]
    ppermute x14 -> x0, starting transfers between devices: 20 us -> none  [swapped(): lax.ppermute(x, axis, [(i, i ^ 1 << bit) for i in range(lax.axis_size(axi...]
    reduce_sum x6 -> x4, other arithmetic: 15.3 us -> 0.69 us  [the longest x1 0.4 us: on_device(): jnp.sum(returned.reshape(expert_count, SHARDS, CAP, model_width).astype(j...]
    another operation x11 -> x0, other arithmetic: 11.8 us -> none  [the longest x10 10.2 us: join_half(): jnp.stack([staying, arrived], axis=1).reshape((-1,) + staying.shape[2:])]
    gather x5 -> x0, local copies, waits for them, and re-layouts: 11.2 us -> none  [the longest x1 3.62 us: on_device(): cache_out = jnp.take(cache_out, target, axis=0)]
  transfers between devices with their start and end apart: 16 -> 1, of which waited for: 7 -> 0; matrix products, arithmetic and copies ran while one was open for 36% -> 3% of each run, Pallas kernels for 0% -> 67%
where the time goes in v1:
time: 129 us; the launch traced here: 128 us
  Pallas kernels  85.6 us (66%)
  blocking collectives  20.4 us (16%)
  local copies, waits for them, and re-layouts  10.2 us (8%)
  matrix products  4.31 us (3%)
  starting transfers between devices  3.8 us (3%)
  other arithmetic  2.87 us (2%)
    pallas_call x1, Pallas kernels, attention(): pl.pallas_call(attend_kernel, out_shape=jax.ShapeDtypeStruct(q.shape, bf)...  85.6 us
    all_to_all x1, blocking collectives, on_device(): lax.all_to_all(copies, ('branch', 'expert'), split_axis=0, concat_axis=0,...  20.4 us
    all_to_all x1, starting transfers between devices, on_device(): lax.all_to_all(jnp.dot(hidden, w_down[0], preferred_element_type=jnp.floa...  3.8 us
    unnamed x16, local copies, waits for them, and re-layouts  3.29 us
  transfers between devices with their start and end apart: 1, of which 0 were waited for; matrix products, arithmetic and copies ran while one was open for 3% of the time, Pallas kernels for 67%

profile of v1, /device:TPU:0, one launch (start us, length us, event | category | flops | bytes accessed | tf_op | source)
XLA Modules:
  0.0 128.1 jit_solution(12148676940555800374)
XLA Ops:
  0.6 0.0 copy-start
  0.7 0.9 copy.26
  1.6 0.8 copy.27
  2.3 0.1 multiply_reduce_fusion.1
  2.4 1.0 reshape.131
  3.5 0.2 convolution_convert_fusion.1
  3.7 0.2 broadcast_in_dim.5
  3.9 20.4 %all_to_all.10 = bf16[16,2,7168]{2,1,0:T(2,128)(2,1)S(1)} all-to-all(bf16[16,2,7168]{2,1,0:T(2,128)(2,1)S(1)} %bitcast.39), channel_id=1, replica_groups=mesh['group'=2,'branch'=8,'expert'=2] {'branch','expert'}, dimensions={0} | all-to-all | bytes 917504 | tf_op jit(solution)/shard_map/all_to_all | solution.py:341
  24.4 0.2 reshape.133
  24.5 1.9 %fusion.3 = f32[32,128]{1,0:T(8,128)S(1)} fusion(bf16[32,7168]{1,0:T(8,128)(2,1)S(1)} %reshape.133, bf16[1,7168,128]{2,1,0:T(8,128)(2,1)} %param.23), kind=kOutput, calls=%fused_computation.5 | convolution fusion | flops 58720256 | bytes 2310144 | tf_op jit(solution)/shard_map/dot_general | solution.py:343
  26.4 0.0 copy-done
  26.4 2.3 %convolution_convert_fusion = bf16[32,7168]{1,0:T(8,128)(2,1)S(1)} fusion(bf16[1,128,7168]{2,1,0:T(8,128)(2,1)S(1)} %copy-done, bf16[32,7168]{1,0:T(8,128)(2,1)S(1)} %reshape.133, bf16[1,7168,128]{2,1,0:T(8,128)(2,1)} %param.24, f32[32,128]{1,0:T(8,128)S(1)} %fusion.3), kind=kOutput, calls=%fused_computation | convolution fusion | flops 117694464 | bytes 4603904 | tf_op jit(solution)/shard_map/dot_general | solution.py:347
  28.7 0.0 copy-start.2
  28.7 0.0 copy-start.1
  28.7 0.9 reshape.134
  29.7 3.8 %all-to-all-start.1 = ((bf16[16,2,7168]{2,1,0:T(2,128)(2,1)}), bf16[16,2,7168]{2,1,0:T(2,128)(2,1)S(1)}, u32[]{:S(2)}, u32[]{:S(2)}) async-start(bf16[16,2,7168]{2,1,0:T(2,128)(2,1)} %reshape.134), calls=%async_computation.1 | async-start | bytes 917504 | tf_op jit(solution)/shard_map/all_to_all | solution.py:346
  33.5 0.0 copy-done.2
  33.5 0.0 copy-start.6
  33.5 0.0 copy-start.3
  33.5 0.0 copy-start.4
  33.6 0.1 squeeze.19
  33.7 0.1 squeeze.20
  33.8 0.0 copy-done.1
  33.8 0.2 copy.23
  34.0 0.5 reshape.128
  34.5 0.2 copy.24
  34.8 0.9 copy.25.rope_ref
  35.6 0.0 copy-done.6
  35.6 0.0 copy-start.5
  35.6 0.6 select_reduce_fusion.1.ordering_ref
  36.3 0.0 copy-done.3
  36.3 0.0 copy-done.4
  36.3 0.7 fusion.17.new_ref
  37.0 0.8 pad_maximum_fusion.krope_ref
  37.7 0.0 copy-done.5
  37.7 85.6 %shard_map.140 = bf16[8,256,512]{2,1,0:T(8,128)(2,1)} custom-call(s32[8]{0:T(128)} %select_reduce_fusion.1.ordering_ref, s32[8]{0:T(128)} %copy-done.5, bf16[8,256,512]{2,1,0:T(8,128)(2,1)} %bitcast.37, bf16[8,128,128]{2,1,0:T(8,128)(2,1)} %copy.25.rope_ref, bf16[8,8,640]{2,1,0:T(8,128)(2,1)} %fusion.17.new_ref, bf16[1024,512]{1,0:T(8,128)(2,1)} %bitcast.41, ...), custom_call_target="tpu_custom_call" | custom-call | tf_op jit(solution)/shard_map/pallas_call | solution.py:269
  123.3 0.1 eq.75
  123.4 0.1 select_multiply_fusion
  123.5 0.0 all-to-all-done.1
  123.5 0.4 convert_reduce_fusion
  123.9 0.1 mul.97
  124.0 0.2 multiply_reduce_fusion
  124.2 0.8 convert_element_type.58
  125.0 3.1 %copy.29 = bf16[8,2,128,512]{3,2,1,0:T(8,128)(2,1)} copy(bf16[8,2,128,512]{3,2,1,0:T(8,128)(2,1)} %bitcast.36) | data formatting | bytes 4194304
  (10 shorter events, 0.1 us)
Async XLA Ops:
  0.6 25.8 %copy-start = (bf16[1,128,7168]{2,1,0:T(8,128)(2,1)S(1)}, bf16[1,128,7168]{2,1,0:T(8,128)(2,1)}, u32[]{:S(2)}) copy-start(bf16[1,128,7168]{2,1,0:T(8,128)(2,1)} %param.25) | copy-start | bytes 5505028
  28.7 4.8 %copy-start.2 = (bf16[1,128,512]{2,1,0:T(8,128)(2,1)S(1)}, bf16[1,128,512]{2,1,0:T(8,128)(2,1)}, u32[]{:S(2)}) copy-start(bf16[1,128,512]{2,1,0:T(8,128)(2,1)} %param.14) | copy-start | bytes 393220
  28.7 5.1 %copy-start.1 = (bf16[8,2,8192]{2,1,0:T(2,128)(2,1)S(1)}, bf16[8,2,8192]{2,1,0:T(2,128)(2,1)}, u32[]{:S(2)}) copy-start(bf16[8,2,8192]{2,1,0:T(2,128)(2,1)} %param.16) | copy-start | bytes 786436
  29.7 93.8 %all-to-all-start.1 = ((bf16[16,2,7168]{2,1,0:T(2,128)(2,1)}), bf16[16,2,7168]{2,1,0:T(2,128)(2,1)S(1)}, u32[]{:S(2)}, u32[]{:S(2)}) async-start(bf16[16,2,7168]{2,1,0:T(2,128)(2,1)} %reshape.134), calls=%async_computation.1 | async-start | bytes 917504 | tf_op jit(solution)/shard_map/all_to_all | solution.py:346
  33.5 2.1 %copy-start.6 = (s32[8]{0:T(128)S(1)}, s32[8]{0:T(128)}, u32[]{:S(2)}) copy-start(s32[8]{0:T(128)} %param.19) | copy-start | bytes 100
  33.5 2.8 %copy-start.3 = (bf16[8,2,512]{2,1,0:T(2,128)(2,1)S(1)}, bf16[8,2,512]{2,1,0:T(2,128)(2,1)}, u32[]{:S(2)}) copy-start(bf16[8,2,512]{2,1,0:T(2,128)(2,1)} %param.17) | copy-start | bytes 49156
  33.5 2.8 %copy-start.4 = (bf16[8,2,64]{2,1,0:T(2,128)(2,1)S(1)}, bf16[8,2,64]{2,1,0:T(2,128)(2,1)}, u32[]{:S(2)}) copy-start(bf16[8,2,64]{2,1,0:T(2,128)(2,1)} %param.18) | copy-start | bytes 6148
  35.6 2.1 %copy-start.5 = (s32[8]{0:T(128)}, s32[8]{0:T(128)S(1)}, u32[]{:S(2)}) copy-start(s32[8]{0:T(128)S(1)} %broadcast_xor_fusion.target_ref) | copy-start | bytes 100

commit v2 on v1

--- a/solution.py
+++ b/solution.py
@@ -24,13 +24,17 @@
 
 def attend_kernel(
     ordering_ref,
-    target_ref,
     q_ref,
     rope_ref,
     new_ref,
     keys_ref,
     krope_ref,
-    out_ref,
+    blocks_ref,
+    w_gate_ref,
+    w_up_ref,
+    w_down_ref,
+    answers,
+    sums_ref,
     q_send,
     rope_send,
     new_send,
@@ -41,7 +45,33 @@
     kpack,
     kdup,
     result,
-    answers,
+    w_gate,
+    w_up,
+    w_down,
+    cross_in,
+    mixed,
+    mixed_in,
+    sib_mixed,
+    stacked,
+    part_out,
+    part_in,
+    pair_sum,
+    pair_in,
+    final,
+    load_sem,
+    local_sem,
+    cross_send,
+    cross_recv,
+    mix_send,
+    mix_recv,
+    mixsib_send,
+    mixsib_recv,
+    y_send,
+    y_recv,
+    pair_send,
+    pair_recv,
+    ret_send,
+    ret_recv,
     sib_send,
     sib_recv,
     part_send,
@@ -73,12 +103,32 @@
     def peer(x):
         return place(flipped(branch, x % HALF, 3), core)
 
+    experts = blocks_ref.shape[0]
+    block_rows = blocks_ref.shape[1]
+    mine = branch // HALF
+
+    def across(d):
+        return (mine + d) % experts
+
+    def far(d):
+        return place(across(d) * HALF + branch % HALF, core)
+
+    loads = [
+        pltpu.make_async_copy(src, dst, load_sem.at[i])
+        for i, (src, dst) in enumerate(
+            [(w_gate_ref, w_gate), (w_up_ref, w_up), (w_down_ref, w_down)]
+        )
+    ]
+    for copy in loads:
+        copy.start()
     barrier = pltpu.get_barrier_semaphore()
-    for other in [sibling, partner] + [peer(j) for j in range(1, HALF)]:
+    for other in (
+        [sibling] + [peer(j) for j in range(1, HALF)] + [far(d) for d in range(1, experts)]
+    ):
         pl.semaphore_signal(
             barrier, inc=1, device_id=other, device_id_type=pl.DeviceIdType.MESH
         )
-    pl.semaphore_wait(barrier, 2 + HALF - 1)
+    pl.semaphore_wait(barrier, HALF + experts - 1)
 
     def remote(src, dst, send, recv, where):
         return pltpu.make_async_remote_copy(
@@ -135,12 +185,91 @@
     def answer_copy(x):
         return remote(result.at[x], answers.at[x], ans_send.at[x], ans_recv.at[x], peer(x))
 
+    def cross_copy(d):
+        return remote(
+            blocks_ref.at[across(d)], cross_in.at[d], cross_send.at[d], cross_recv.at[d], far(d)
+        )
+
+    def mix_copy(j):
+        return remote(mixed, mixed_in.at[j], mix_send.at[j], mix_recv.at[j], peer(j))
+
+    def mixsib_copy(j):
+        source = mixed if j == 0 else mixed_in.at[j]
+        return remote(source, sib_mixed.at[j], mixsib_send.at[j], mixsib_recv.at[j], sibling)
+
+    def y_copy(j):
+        return remote(part_out.at[j], part_in.at[j], y_send.at[j], y_recv.at[j], sibling)
+
+    def pair_copy(j):
+        return remote(pair_sum.at[j], pair_in.at[j], pair_send.at[j], pair_recv.at[j], peer(j))
+
+    def ret_copy(d):
+        return remote(final, sums_ref.at[mine], ret_send.at[d], ret_recv.at[d], far(d))
+
+    own_sums = pltpu.make_async_copy(final, sums_ref.at[mine], local_sem.at[2])
+
+    def mix_blocks():
+        total = blocks_ref[mine].astype(jnp.float32)
+        for d in range(1, experts):
+            cross_copy(d).wait_recv()
+            total = total + cross_in[d].astype(jnp.float32)
+        mixed[...] = total.astype(jnp.bfloat16)
+        for j in (2, 3, 1):
+            mix_copy(j).start()
+
+    def share_blocks():
+        mixsib_copy(0).start()
+        for j in range(1, HALF):
+            mix_copy(j).wait_recv()
+            mixsib_copy(j).start()
+
+    def feed_forward():
+        for j in range(0, HALF):
+            mixsib_copy(j).wait_recv()
+        for copy in loads:
+            copy.wait()
+        pieces = [mixed[...]] + [mixed_in[j] for j in range(1, HALF)]
+        pieces = pieces + [sib_mixed[j] for j in range(HALF)]
+        for i in range(0, 2 * HALF, 2):
+            two = jnp.concatenate([p.astype(jnp.float32) for p in pieces[i : i + 2]], axis=0)
+            stacked[pl.ds(i * block_rows, 2 * block_rows)] = two.astype(jnp.bfloat16)
+        gate = jnp.dot(stacked[...], w_gate[...], preferred_element_type=jnp.float32)
+        lifted = jnp.dot(stacked[...], w_up[...], preferred_element_type=jnp.float32)
+        hidden = (gate / (1.0 + jnp.exp(-gate)) * lifted).astype(jnp.bfloat16)
+        parts = jnp.dot(hidden, w_down[...], preferred_element_type=jnp.float32)
+        for j in range(HALF):
+            own_at, sib_at = j * block_rows, (HALF + j) * block_rows
+            pair_sum[j] = parts[own_at : own_at + block_rows].astype(jnp.bfloat16)
+            part_out[j] = parts[sib_at : sib_at + block_rows].astype(jnp.bfloat16)
+            y_copy(j).start()
+
+    def add_pairs():
+        for j in (2, 3, 1, 0):
+            y_copy(j).wait_recv()
+            pair_sum[j] = (
+                pair_sum[j].astype(jnp.float32) + part_in[j].astype(jnp.float32)
+            ).astype(jnp.bfloat16)
+            if j:
+                pair_copy(j).start()
+
+    def finish_sums():
+        total = pair_sum[0].astype(jnp.float32)
+        for j in range(1, HALF):
+            pair_copy(j).wait_recv()
+            total = total + pair_in[j].astype(jnp.float32)
+        final[...] = total.astype(jnp.bfloat16)
+        own_sums.start()
+        for d in range(1, experts):
+            ret_copy(d).start()
+
     def gather(x, to_q, to_rope, to_new):
         at = ordering_ref[x]
         to_q[x] = q_ref[at]
         to_rope[x] = rope_ref[at]
         to_new[x] = new_ref[at]
 
+    for d in range(1, experts):
+        cross_copy(d).start()
     for copy in sib_copies():
         copy.start()
     order = [2, 3, 6, 7]
@@ -156,6 +285,8 @@
             gather(y, q_send, rope_send, new_send)
             for copy in query_copies(y):
                 copy.start()
+        if c == 1:
+            mix_blocks()
     for x in (0, HALF):
         gather(x, q_in, rope_in, new_in)
 
@@ -210,9 +341,14 @@
         summed = summed + w0 * entries[0:1] + w1 * entries[1:2]
         return (summed / total).astype(jnp.bfloat16)
 
-    def run(start, *cache):
-        answers[start] = attend(start, *cache)
-
+    def local_copy(i):
+        return pltpu.make_async_copy(result.at[i * HALF], answers.at[i * HALF], local_sem.at[i])
+
+    def run_local(i, *cache):
+        result[i * HALF] = attend(i * HALF, *cache)
+        local_copy(i).start()
+
+    def run(start, stop, *cache):
         def body(x, carry):
             for copy in query_copies(x):
                 copy.wait_recv()
@@ -220,13 +356,19 @@
             answer_copy(x).start()
             return carry
 
-        lax.fori_loop(start + 1, start + HALF, body, 0)
+        lax.fori_loop(start, stop, body, 0)
 
     spread(krope_ref[...], 0)
     for copy in sib_copies():
         copy.wait_recv()
     spread(kpack[0], 1)
-    run(0, keys_ref, kdup.at[0], keys.at[0], kdup.at[1])
+    near = (keys_ref, kdup.at[0], keys.at[0], kdup.at[1])
+    run_local(0, *near)
+    share_blocks()
+    run(1, HALF, *near)
+    feed_forward()
+    add_pairs()
+    finish_sums()
 
     for c in range(CHUNKS):
         for copy in part_copies(c):
@@ -238,13 +380,27 @@
         for copy in fwd_copies(c):
             copy.wait_recv()
     spread(kpack[2], 3)
-    run(HALF, keys.at[1], kdup.at[2], keys.at[2], kdup.at[3])
+    distant = (keys.at[1], kdup.at[2], keys.at[2], kdup.at[3])
+    run(HALF + 1, 2 * HALF, *distant)
+    run_local(1, *distant)
 
     for x in range(tok):
         if x % HALF:
             answer_copy(x).wait_recv()
-    for t in range(tok):
-        out_ref[t] = answers[target_ref[t]]
+    for d in range(1, experts):
+        ret_copy(d).wait_recv()
+    own_sums.wait()
+    for i in range(2):
+        local_copy(i).wait()
+    for d in range(1, experts):
+        cross_copy(d).wait_send()
+        ret_copy(d).wait_send()
+    for j in range(HALF):
+        mixsib_copy(j).wait_send()
+        y_copy(j).wait_send()
+        if j:
+            mix_copy(j).wait_send()
+            pair_copy(j).wait_send()
     for copy in sib_copies():
         copy.wait_send()
     for c in range(CHUNKS):
@@ -257,7 +413,7 @@
             answer_copy(x).wait_send()
 
 
-def attention(ordering, target, q, rope, new, keys, krope):
+def attention(ordering, q, rope, new, keys, krope, blocks, w_gate, w_up, w_down):
     tok, rows, lat = q.shape
     heads, lanes = rope.shape[1:]
     half_len = keys.shape[0]
@@ -265,12 +421,16 @@
     bf = jnp.bfloat16
     vmem = pl.BlockSpec(memory_space=pltpu.VMEM)
     smem = pl.BlockSpec(memory_space=pltpu.SMEM)
+    anywhere = pl.BlockSpec(memory_space=pl.ANY)
     dma = pltpu.SemaphoreType.DMA
+    experts, block_rows, width = blocks.shape
+    quad = pltpu.VMEM((HALF, block_rows, width), bf)
+    block = pltpu.VMEM((block_rows, width), bf)
     return pl.pallas_call(
         attend_kernel,
-        out_shape=jax.ShapeDtypeStruct(q.shape, bf),
-        in_specs=[smem, smem] + [vmem] * 5,
-        out_specs=vmem,
+        out_shape=(jax.ShapeDtypeStruct(q.shape, bf), jax.ShapeDtypeStruct(blocks.shape, bf)),
+        in_specs=[smem] + [vmem] * 6 + [anywhere] * 3,
+        out_specs=(anywhere, anywhere),
         scratch_shapes=[
             pltpu.VMEM(q.shape, bf),
             pltpu.VMEM(rope.shape, bf),
@@ -282,7 +442,33 @@
             pltpu.VMEM((3, packed_len, lanes), bf),
             pltpu.VMEM((4, half_len, lanes), bf),
             pltpu.VMEM(q.shape, bf),
-            pltpu.VMEM(q.shape, bf),
+            pltpu.VMEM(w_gate.shape, bf),
+            pltpu.VMEM(w_up.shape, bf),
+            pltpu.VMEM(w_down.shape, bf),
+            pltpu.VMEM((experts, block_rows, width), bf),
+            block,
+            quad,
+            quad,
+            pltpu.VMEM((2 * HALF * block_rows, width), bf),
+            quad,
+            quad,
+            quad,
+            quad,
+            block,
+            dma((3,)),
+            dma((3,)),
+            dma((experts,)),
+            dma((experts,)),
+            dma((HALF,)),
+            dma((HALF,)),
+            dma((HALF,)),
+            dma((HALF,)),
+            dma((HALF,)),
+            dma((HALF,)),
+            dma((HALF,)),
+            dma((HALF,)),
+            dma((experts,)),
+            dma((experts,)),
             dma((2,)),
             dma((2,)),
             dma((2, CHUNKS)),
@@ -297,7 +483,41 @@
         compiler_params=pltpu.CompilerParams(
             collective_id=0, has_side_effects=True, vmem_limit_bytes=56 * 1024 * 1024
         ),
-    )(ordering, target, q, rope, new, keys, krope)
+    )(ordering, q, rope, new, keys, krope, blocks, w_gate, w_up, w_down)
+
+
+def reorder_kernel(target_ref, source, out, held, read, write):
+    tok = held.shape[0]
+
+    def reading(t):
+        return pltpu.make_async_copy(source.at[target_ref[t]], held.at[t], read.at[t])
+
+    def writing(t):
+        return pltpu.make_async_copy(held.at[t], out.at[t], write.at[t])
+
+    for t in range(tok):
+        reading(t).start()
+    for t in range(tok):
+        reading(t).wait()
+        writing(t).start()
+    for t in range(tok):
+        writing(t).wait()
+
+
+def reordered(target, source):
+    anywhere = pl.BlockSpec(memory_space=pl.ANY)
+    tok = source.shape[0]
+    return pl.pallas_call(
+        reorder_kernel,
+        out_shape=jax.ShapeDtypeStruct(source.shape, source.dtype),
+        in_specs=[pl.BlockSpec(memory_space=pltpu.SMEM), anywhere],
+        out_specs=anywhere,
+        scratch_shapes=[
+            pltpu.VMEM(source.shape, source.dtype),
+            pltpu.SemaphoreType.DMA((tok,)),
+            pltpu.SemaphoreType.DMA((tok,)),
+        ],
+    )(target, source)
 
 
 def on_device(
@@ -321,42 +541,27 @@
     model_width = moe_input.shape[-1]
     tok_total = tok_rows * step_count
     expert_count = lax.axis_size("branch") * lax.axis_size("expert") // SHARDS
-    slots = expert_count * CAP
+    block_rows = -(-expert_count * CAP // 8) * 8
     flat = routes.reshape(tok_total, -1)
     chosen = (flat[:, :, None] == jnp.arange(expert_count, dtype=jnp.int32)).astype(jnp.float32)
     gate = jnp.sum(chosen * route_gate.reshape(tok_total, -1, 1), axis=1)
     hit = jnp.sum(chosen, axis=1)
     earlier = (jnp.arange(tok_total)[:, None] > jnp.arange(tok_total)[None, :]).astype(jnp.float32)
     position = jnp.sum(earlier[:, :, None] * hit[None], axis=1)
-    placing = hit[:, :, None] * (position[:, :, None] == jnp.arange(CAP, dtype=jnp.float32))
-    weights = (placing * gate[:, :, None]).reshape(tok_total, slots)
-    placing = placing.reshape(tok_total, slots).astype(jnp.bfloat16)
-    tokens_flat = moe_input.reshape(tok_total, model_width)
-    outgoing = lax.dot_general(
-        placing, tokens_flat, (((0,), (0,)), ((), ())), preferred_element_type=jnp.float32
-    ).astype(jnp.bfloat16)
-    outgoing = outgoing.reshape(expert_count, 1, CAP, model_width)
-    copies = jnp.broadcast_to(outgoing, (expert_count, SHARDS, CAP, model_width))
-    copies = copies.reshape(expert_count * SHARDS, CAP, model_width)
-    arrived = lax.all_to_all(copies, ("branch", "expert"), split_axis=0, concat_axis=0, tiled=True)
-    flattened = arrived.reshape(-1, model_width)
-    gate_value = jnp.dot(flattened, w_gate[0], preferred_element_type=jnp.float32)
-    lifted = jnp.dot(flattened, w_up[0], preferred_element_type=jnp.float32)
-    hidden = (jax.nn.silu(gate_value) * lifted).astype(jnp.bfloat16)
-    returned = lax.all_to_all(
-        jnp.dot(hidden, w_down[0], preferred_element_type=jnp.float32)
+    slot = jnp.arange(block_rows) - CAP * (lax.axis_index("branch") // HALF)
+    placing = hit[:, :, None] * (position[:, :, None] == slot.astype(jnp.float32))
+    weights = (placing * gate[:, :, None]).reshape(tok_total, -1)
+    placing = placing.reshape(tok_total, -1).astype(jnp.bfloat16)
+    blocks = (
+        lax.dot_general(
+            placing,
+            moe_input.reshape(tok_total, model_width),
+            (((0,), (0,)), ((), ())),
+            preferred_element_type=jnp.float32,
+        )
         .astype(jnp.bfloat16)
-        .reshape(arrived.shape),
-        ("branch", "expert"),
-        split_axis=0,
-        concat_axis=0,
-        tiled=True,
+        .reshape(expert_count, block_rows, model_width)
     )
-    expert_sums = jnp.sum(
-        returned.reshape(expert_count, SHARDS, CAP, model_width).astype(jnp.float32), axis=1
-    ).reshape(slots, model_width)
-    combined = jnp.sum(weights[:, :, None] * expert_sums[None], axis=1)
-    moe_out = combined.astype(jnp.bfloat16).reshape(tok_rows, step_count, model_width)
 
     counting = jnp.arange(tok_rows, dtype=jnp.int32)
     own_index = lax.axis_index("branch") % tok_rows
@@ -369,16 +574,27 @@
     new = jnp.pad(new, ((0, 0), (0, 8 - step_count), (0, 0)))
     krope = rope_cache[0].reshape(2, -1, rope_width)
     krope = jnp.concatenate([krope[0], krope[1]], axis=-1)
-    attended = attention(
+    answers, sums = attention(
         ordering,
-        target,
         q_latent.reshape(tok_rows, step_count * head_count, lat),
         rope,
         new,
         latent_cache[0],
         krope,
+        blocks,
+        w_gate[0],
+        w_up[0],
+        w_down[0],
     )
-    attended = attended.reshape(q_latent.shape)
+    attended = reordered(target, answers).reshape(q_latent.shape)
+    moe_out = lax.dot_general(
+        weights,
+        sums.reshape(-1, model_width).astype(jnp.float32),
+        (((1,), (0,)), ((), ())),
+        precision=lax.Precision.HIGHEST,
+        preferred_element_type=jnp.float32,
+    )
+    moe_out = moe_out.astype(jnp.bfloat16).reshape(tok_rows, step_count, model_width)
     return (attended, moe_out)
 
 

time: 129 us -> 119 us (0.922)
  Pallas kernels: 85.6 us -> 107 us
  blocking collectives: 20.4 us -> 0 us
  local copies, waits for them, and re-layouts: 10.2 us -> 6.24 us
  starting transfers between devices: 3.8 us -> 0 us
  matrix products: 4.31 us -> 1.41 us
    pallas_call x1 -> x2, Pallas kernels: 85.6 us -> 107 us  [the longest x1 104 us: attention(): pl.pallas_call(attend_kernel, out_shape=(jax.ShapeDtypeStruct(q.shape, bf...]
    all_to_all x1 -> x0, blocking collectives: 20.4 us -> none  [on_device(): lax.all_to_all(copies, ('branch', 'expert'), split_axis=0, concat_axis=0,...]
    all_to_all x1 -> x0, starting transfers between devices: 3.8 us -> none  [on_device(): lax.all_to_all(jnp.dot(hidden, w_down[0], preferred_element_type=jnp.floa...]
    unnamed x16 -> x7, local copies, waits for them, and re-layouts: 3.29 us -> 0.16 us
    dot_general x3 -> x2, matrix products: 4.31 us -> 1.41 us  [the longest x1 0.95 us: on_device(): lax.dot_general(placing, moe_input.reshape(tok_total, model_width), (((0,...]
  transfers between devices with their start and end apart: 1 -> 0, of which waited for: 0 -> 0; matrix products, arithmetic and copies ran while one was open for 3% -> 0% of each run, Pallas kernels for 67% -> 0%
where the time goes in v2:
time: 119 us
  Pallas kernels  107 us (90%)
  local copies, waits for them, and re-layouts  6.24 us (5%)
  other arithmetic  3.7 us (3%)
  matrix products  1.41 us (1%)
    pallas_call x1, Pallas kernels, attention(): pl.pallas_call(attend_kernel, out_shape=(jax.ShapeDtypeStruct(q.shape, bf...  104 us
    pallas_call x1, Pallas kernels, reordered(): pl.pallas_call(reorder_kernel, out_shape=jax.ShapeDtypeStruct(source.shap...  3.19 us

profile of v2, /device:TPU:0, one launch (start us, length us, event | category | flops | bytes accessed | tf_op | source)
XLA Modules:
  0.0 118.8 jit_solution(6402259139283128557)
XLA Ops:
  0.6 0.0 copy-start
  0.7 0.7 broadcast_xor_fusion.target_ref
  1.4 0.0 copy-start.2
  1.4 0.7 select_reduce_fusion.1.ordering_ref
  2.0 0.8 copy.23
  2.8 0.8 copy.25
  3.6 0.1 multiply_reduce_fusion
  3.7 1.5 %fusion.6.new_ref = bf16[8,8,640]{2,1,0:T(8,128)(2,1)} fusion(bf16[8,2,64]{2,1,0:T(2,128)(2,1)} %param.18, bf16[8,2,512]{2,1,0:T(2,128)(2,1)} %param.17), kind=kLoop, calls=%fused_computation.10 | loop fusion | flops 409600 | bytes 100352 | tf_op jit(solution)/shard_map/concatenate | solution.py:573
  5.2 0.9 fusion.21
  6.0 0.1 squeeze.19
  6.2 0.1 squeeze.20
  6.3 0.8 pad_maximum_fusion.krope_ref
  7.1 1.0 reshape.97
  8.1 0.9 fusion.1.blocks_ref
  9.0 0.0 copy-done
  9.0 0.2 copy.21
  9.2 0.5 reshape.95
  9.7 0.2 copy.22
  10.0 0.0 copy-done.2
  10.0 0.9 copy.24.rope_ref
  10.8 103.5 %shard_map.140 = (bf16[8,256,512]{2,1,0:T(8,128)(2,1)}, bf16[2,8,7168]{2,1,0:T(8,128)(2,1)}) custom-call(s32[8]{0:T(128)} %select_reduce_fusion.1.ordering_ref, bf16[8,256,512]{2,1,0:T(8,128)(2,1)} %bitcast.25, bf16[8,128,128]{2,1,0:T(8,128)(2,1)} %copy.24.rope_ref, bf16[8,8,640]{2,1,0:T(8,128)(2,1)} %fusion.6.new_ref, bf16[1024,512]{1,0:T(8,128)(2,1)} %bitcast.29, ...), custom_call_target="tpu_custom_call" | custom-call | tf_op jit(solution)/shard_map/pallas_call | solution.py:429
  114.4 0.0 copy-start.1
  114.4 3.2 %shard_map.141 = bf16[8,256,512]{2,1,0:T(8,128)(2,1)} custom-call(s32[8]{0:T(128)} %copy-done.2, bf16[8,256,512]{2,1,0:T(8,128)(2,1)} %get-tuple-element.4.source), custom_call_target="tpu_custom_call" | custom-call | tf_op jit(solution)/shard_map/pallas_call | solution.py:510
  117.6 0.0 copy-done.1
  117.6 0.5 fusion
  118.1 0.8 reshape.100
  (3 shorter events, 0.0 us)
Async XLA Ops:
  0.6 8.4 %copy-start = (bf16[8,2,8192]{2,1,0:T(2,128)(2,1)S(1)}, bf16[8,2,8192]{2,1,0:T(2,128)(2,1)}, u32[]{:S(2)}) copy-start(bf16[8,2,8192]{2,1,0:T(2,128)(2,1)} %param.16) | copy-start | bytes 786436
  1.4 8.6 %copy-start.2 = (s32[8]{0:T(128)}, s32[8]{0:T(128)S(1)}, u32[]{:S(2)}) copy-start(s32[8]{0:T(128)S(1)} %broadcast_xor_fusion.target_ref) | copy-start | bytes 100
  114.4 3.2 %copy-start.1 = (bf16[2,8,7168]{2,1,0:T(8,128)(2,1)S(1)}, bf16[2,8,7168]{2,1,0:T(8,128)(2,1)}, u32[]{:S(2)}) copy-start(bf16[2,8,7168]{2,1,0:T(8,128)(2,1)} %get-tuple-element.5) | copy-start | bytes 688132

commit v3 on v2

--- a/solution.py
+++ b/solution.py
@@ -23,7 +23,7 @@
 
 
 def attend_kernel(
-    ordering_ref,
+    slot_ref,
     q_ref,
     rope_ref,
     new_ref,
@@ -53,6 +53,7 @@
     mixed_in,
     sib_mixed,
     stacked,
+    part_own,
     part_out,
     part_in,
     pair_sum,
@@ -204,16 +205,15 @@
         return remote(pair_sum.at[j], pair_in.at[j], pair_send.at[j], pair_recv.at[j], peer(j))
 
     def ret_copy(d):
-        return remote(final, sums_ref.at[mine], ret_send.at[d], ret_recv.at[d], far(d))
-
-    own_sums = pltpu.make_async_copy(final, sums_ref.at[mine], local_sem.at[2])
+        return remote(final.at[d], sums_ref.at[mine], ret_send.at[d], ret_recv.at[d], far(experts - d))
+
+    own_sums = pltpu.make_async_copy(final.at[0], sums_ref.at[mine], local_sem.at[2])
 
     def mix_blocks():
-        total = blocks_ref[mine].astype(jnp.float32)
+        mixed[0] = blocks_ref[mine]
         for d in range(1, experts):
             cross_copy(d).wait_recv()
-            total = total + cross_in[d].astype(jnp.float32)
-        mixed[...] = total.astype(jnp.bfloat16)
+            mixed[d] = cross_in[d]
         for j in (2, 3, 1):
             mix_copy(j).start()
 
@@ -228,32 +228,32 @@
             mixsib_copy(j).wait_recv()
         for copy in loads:
             copy.wait()
-        pieces = [mixed[...]] + [mixed_in[j] for j in range(1, HALF)]
-        pieces = pieces + [sib_mixed[j] for j in range(HALF)]
-        for i in range(0, 2 * HALF, 2):
-            two = jnp.concatenate([p.astype(jnp.float32) for p in pieces[i : i + 2]], axis=0)
-            stacked[pl.ds(i * block_rows, 2 * block_rows)] = two.astype(jnp.bfloat16)
+        pieces = [mixed] + [mixed_in.at[j] for j in range(1, HALF)]
+        pieces = pieces + [sib_mixed.at[j] for j in range(HALF)]
+        rows_of = [p[d].astype(jnp.float32) for p in pieces for d in range(experts)]
+        stacked[...] = jnp.concatenate(rows_of, axis=0).astype(jnp.bfloat16)
         gate = jnp.dot(stacked[...], w_gate[...], preferred_element_type=jnp.float32)
         lifted = jnp.dot(stacked[...], w_up[...], preferred_element_type=jnp.float32)
         hidden = (gate / (1.0 + jnp.exp(-gate)) * lifted).astype(jnp.bfloat16)
         parts = jnp.dot(hidden, w_down[...], preferred_element_type=jnp.float32)
         for j in range(HALF):
-            own_at, sib_at = j * block_rows, (HALF + j) * block_rows
-            pair_sum[j] = parts[own_at : own_at + block_rows].astype(jnp.bfloat16)
-            part_out[j] = parts[sib_at : sib_at + block_rows].astype(jnp.bfloat16)
+            for d in range(experts):
+                own_at = (j * experts + d) * block_rows
+                sib_at = own_at + HALF * experts * block_rows
+                part_own[j, d] = parts[own_at : own_at + block_rows]
+                part_out[j, d] = parts[sib_at : sib_at + block_rows]
             y_copy(j).start()
 
     def add_pairs():
         for j in (2, 3, 1, 0):
             y_copy(j).wait_recv()
-            pair_sum[j] = (
-                pair_sum[j].astype(jnp.float32) + part_in[j].astype(jnp.float32)
-            ).astype(jnp.bfloat16)
+            part_own[j] = part_own[j] + part_in[j]
+            pair_sum[j] = part_own[j].astype(jnp.bfloat16)
             if j:
                 pair_copy(j).start()
 
     def finish_sums():
-        total = pair_sum[0].astype(jnp.float32)
+        total = part_own[0]
         for j in range(1, HALF):
             pair_copy(j).wait_recv()
             total = total + pair_in[j].astype(jnp.float32)
@@ -263,7 +263,10 @@
             ret_copy(d).start()
 
     def gather(x, to_q, to_rope, to_new):
-        at = ordering_ref[x]
+        want = flipped(branch % tok, x, 3)
+        at = 0
+        for t in range(tok):
+            at = jnp.where(slot_ref[t] == want, t, at)
         to_q[x] = q_ref[at]
         to_rope[x] = rope_ref[at]
         to_new[x] = new_ref[at]
@@ -368,7 +371,6 @@
     run(1, HALF, *near)
     feed_forward()
     add_pairs()
-    finish_sums()
 
     for c in range(CHUNKS):
         for copy in part_copies(c):
@@ -381,6 +383,7 @@
             copy.wait_recv()
     spread(kpack[2], 3)
     distant = (keys.at[1], kdup.at[2], keys.at[2], kdup.at[3])
+    finish_sums()
     run(HALF + 1, 2 * HALF, *distant)
     run_local(1, *distant)
 
@@ -413,7 +416,7 @@
             answer_copy(x).wait_send()
 
 
-def attention(ordering, q, rope, new, keys, krope, blocks, w_gate, w_up, w_down):
+def attention(slots, q, rope, new, keys, krope, blocks, w_gate, w_up, w_down):
     tok, rows, lat = q.shape
     heads, lanes = rope.shape[1:]
     half_len = keys.shape[0]
@@ -424,8 +427,9 @@
     anywhere = pl.BlockSpec(memory_space=pl.ANY)
     dma = pltpu.SemaphoreType.DMA
     experts, block_rows, width = blocks.shape
-    quad = pltpu.VMEM((HALF, block_rows, width), bf)
-    block = pltpu.VMEM((block_rows, width), bf)
+    quad = pltpu.VMEM((HALF, experts, block_rows, width), bf)
+    quad_sum = pltpu.VMEM((HALF, experts, block_rows, width), jnp.float32)
+    block = pltpu.VMEM((experts, block_rows, width), bf)
     return pl.pallas_call(
         attend_kernel,
         out_shape=(jax.ShapeDtypeStruct(q.shape, bf), jax.ShapeDtypeStruct(blocks.shape, bf)),
@@ -449,9 +453,10 @@
             block,
             quad,
             quad,
-            pltpu.VMEM((2 * HALF * block_rows, width), bf),
-            quad,
-            quad,
+            pltpu.VMEM((2 * HALF * experts * block_rows, width), bf),
+            quad_sum,
+            quad_sum,
+            quad_sum,
             quad,
             quad,
             block,
@@ -483,14 +488,21 @@
         compiler_params=pltpu.CompilerParams(
             collective_id=0, has_side_effects=True, vmem_limit_bytes=56 * 1024 * 1024
         ),
-    )(ordering, q, rope, new, keys, krope, blocks, w_gate, w_up, w_down)
-
-
-def reorder_kernel(target_ref, source, out, held, read, write):
+    )(slots, q, rope, new, keys, krope, blocks, w_gate, w_up, w_down)
+
+
+def reorder_kernel(slot_ref, source, out, held, read, write):
     tok = held.shape[0]
+    own = lax.axis_index("branch") % tok
+
+    def chosen(t):
+        at = 0
+        for x in range(tok):
+            at = jnp.where(slot_ref[t] == flipped(own, x, 3), x, at)
+        return at
 
     def reading(t):
-        return pltpu.make_async_copy(source.at[target_ref[t]], held.at[t], read.at[t])
+        return pltpu.make_async_copy(source.at[chosen(t)], held.at[t], read.at[t])
 
     def writing(t):
         return pltpu.make_async_copy(held.at[t], out.at[t], write.at[t])
@@ -504,7 +516,7 @@
         writing(t).wait()
 
 
-def reordered(target, source):
+def reordered(slots, source):
     anywhere = pl.BlockSpec(memory_space=pl.ANY)
     tok = source.shape[0]
     return pl.pallas_call(
@@ -517,7 +529,7 @@
             pltpu.SemaphoreType.DMA((tok,)),
             pltpu.SemaphoreType.DMA((tok,)),
         ],
-    )(target, source)
+    )(slots, source)
 
 
 def on_device(
@@ -541,15 +553,13 @@
     model_width = moe_input.shape[-1]
     tok_total = tok_rows * step_count
     expert_count = lax.axis_size("branch") * lax.axis_size("expert") // SHARDS
-    block_rows = -(-expert_count * CAP // 8) * 8
     flat = routes.reshape(tok_total, -1)
     chosen = (flat[:, :, None] == jnp.arange(expert_count, dtype=jnp.int32)).astype(jnp.float32)
     gate = jnp.sum(chosen * route_gate.reshape(tok_total, -1, 1), axis=1)
     hit = jnp.sum(chosen, axis=1)
     earlier = (jnp.arange(tok_total)[:, None] > jnp.arange(tok_total)[None, :]).astype(jnp.float32)
     position = jnp.sum(earlier[:, :, None] * hit[None], axis=1)
-    slot = jnp.arange(block_rows) - CAP * (lax.axis_index("branch") // HALF)
-    placing = hit[:, :, None] * (position[:, :, None] == slot.astype(jnp.float32))
+    placing = hit[:, :, None] * (position[:, :, None] == jnp.arange(CAP, dtype=jnp.float32))
     weights = (placing * gate[:, :, None]).reshape(tok_total, -1)
     placing = placing.reshape(tok_total, -1).astype(jnp.bfloat16)
     blocks = (
@@ -560,14 +570,9 @@
             preferred_element_type=jnp.float32,
         )
         .astype(jnp.bfloat16)
-        .reshape(expert_count, block_rows, model_width)
+        .reshape(expert_count, CAP, model_width)
     )
 
-    counting = jnp.arange(tok_rows, dtype=jnp.int32)
-    own_index = lax.axis_index("branch") % tok_rows
-    target = jnp.bitwise_xor(own_index, branch_slot)
-    chooser = (target[None, :] == counting[:, None]).astype(jnp.int32)
-    ordering = jnp.sum(chooser * counting[None, :], axis=1)
     rope = q_rope.reshape(tok_rows, step_count, head_count, rope_width)
     rope = rope.transpose(0, 2, 1, 3).reshape(tok_rows, head_count, step_count * rope_width)
     new = jnp.concatenate([new_latent, new_rope, new_rope], axis=-1)
@@ -575,7 +580,7 @@
     krope = rope_cache[0].reshape(2, -1, rope_width)
     krope = jnp.concatenate([krope[0], krope[1]], axis=-1)
     answers, sums = attention(
-        ordering,
+        branch_slot,
         q_latent.reshape(tok_rows, step_count * head_count, lat),
         rope,
         new,
@@ -586,7 +591,7 @@
         w_up[0],
         w_down[0],
     )
-    attended = reordered(target, answers).reshape(q_latent.shape)
+    attended = reordered(branch_slot, answers).reshape(q_latent.shape)
     moe_out = lax.dot_general(
         weights,
         sums.reshape(-1, model_width).astype(jnp.float32),

time: 119 us -> 109 us (0.916)
  Pallas kernels: 107 us -> 97.7 us
  other arithmetic: 3.7 us -> 2.38 us
    pallas_call x1, Pallas kernels: 104 us -> 94.4 us  [attention(): pl.pallas_call(attend_kernel, out_shape=(jax.ShapeDtypeStruct(q.shape, bf...]
where the time goes in v3:
time: 109 us; the launch traced here: 108 us
  Pallas kernels  97.7 us (90%)
  local copies, waits for them, and re-layouts  6.93 us (6%)
  other arithmetic  2.38 us (2%)
    pallas_call x1, Pallas kernels, attention(): pl.pallas_call(attend_kernel, out_shape=(jax.ShapeDtypeStruct(q.shape, bf...  94.4 us
    pallas_call x1, Pallas kernels, reordered(): pl.pallas_call(reorder_kernel, out_shape=jax.ShapeDtypeStruct(source.shap...  3.26 us

profile of v3, /device:TPU:0, one launch (start us, length us, event | category | flops | bytes accessed | tf_op | source)
XLA Modules:
  0.0 108.3 jit_solution(14145580006259173366)
XLA Ops:
  0.6 0.0 copy-start
  0.6 0.8 copy.23
  1.4 0.8 copy.25
  2.2 0.1 multiply_reduce_fusion
  2.3 1.5 %fusion.5.new_ref = bf16[8,8,640]{2,1,0:T(8,128)(2,1)} fusion(bf16[8,2,64]{2,1,0:T(2,128)(2,1)} %param.18, bf16[8,2,512]{2,1,0:T(2,128)(2,1)} %param.17), kind=kLoop, calls=%fused_computation.9 | loop fusion | flops 409600 | bytes 100352 | tf_op jit(solution)/shard_map/concatenate | solution.py:578
  3.8 0.9 fusion.14
  4.7 0.1 squeeze.19
  4.8 0.1 squeeze.20
  5.0 0.8 pad_maximum_fusion.krope_ref
  5.7 1.0 reshape.91
  6.8 0.2 convolution_convert_fusion
  6.9 0.7 reshape.92.blocks_ref
  7.6 0.0 copy-done
  7.6 0.2 copy.21
  7.7 0.5 reshape.89
  8.3 0.2 copy.22
  8.5 0.9 copy.24.rope_ref
  9.4 94.4 %shard_map.140 = (bf16[8,256,512]{2,1,0:T(8,128)(2,1)}, bf16[2,2,7168]{2,1,0:T(2,128)(2,1)}) custom-call(s32[8]{0:T(128)} %slot_ref.3, bf16[8,256,512]{2,1,0:T(8,128)(2,1)} %bitcast.22, bf16[8,128,128]{2,1,0:T(8,128)(2,1)} %copy.24.rope_ref, bf16[8,8,640]{2,1,0:T(8,128)(2,1)} %fusion.5.new_ref, bf16[1024,512]{1,0:T(8,128)(2,1)} %bitcast.27, ...), custom_call_target="tpu_custom_call" | custom-call | tf_op jit(solution)/shard_map/pallas_call | solution.py:433
  103.8 0.0 copy-start.1
  103.8 3.3 %shard_map.141 = bf16[8,256,512]{2,1,0:T(8,128)(2,1)} custom-call(s32[8]{0:T(128)} %slot_ref.3, bf16[8,256,512]{2,1,0:T(8,128)(2,1)} %get-tuple-element.4.source), custom_call_target="tpu_custom_call" | custom-call | tf_op jit(solution)/shard_map/pallas_call | solution.py:522
  107.1 0.0 copy-done.1
  107.1 0.5 fusion
  107.6 0.8 reshape.94
  (3 shorter events, 0.0 us)
Async XLA Ops:
  0.6 7.0 %copy-start = (bf16[8,2,8192]{2,1,0:T(2,128)(2,1)S(1)}, bf16[8,2,8192]{2,1,0:T(2,128)(2,1)}, u32[]{:S(2)}) copy-start(bf16[8,2,8192]{2,1,0:T(2,128)(2,1)} %param.16) | copy-start | bytes 786436
  103.8 3.3 %copy-start.1 = (bf16[2,2,7168]{2,1,0:T(2,128)(2,1)S(1)}, bf16[2,2,7168]{2,1,0:T(2,128)(2,1)}, u32[]{:S(2)}) copy-start(bf16[2,2,7168]{2,1,0:T(2,128)(2,1)} %get-tuple-element.5) | copy-start | bytes 172036

commit v4 on v3

--- a/solution.py
+++ b/solution.py
@@ -352,14 +352,15 @@
         local_copy(i).start()
 
     def run(start, stop, *cache):
-        def body(x, carry):
+        def body(i, carry):
+            x = start + (i + 1) % (stop - start)
             for copy in query_copies(x):
                 copy.wait_recv()
             result[x] = attend(x, *cache)
             answer_copy(x).start()
             return carry
 
-        lax.fori_loop(start, stop, body, 0)
+        lax.fori_loop(0, stop - start, body, 0)
 
     spread(krope_ref[...], 0)
     for copy in sib_copies():

time: 109 us -> 111 us (1.018)
  Pallas kernels: 97.7 us -> 99.7 us
    pallas_call x1, Pallas kernels: 94.4 us -> 96.5 us  [attention(): pl.pallas_call(attend_kernel, out_shape=(jax.ShapeDtypeStruct(q.shape, bf...]
where the time goes in v4:
time: 111 us; the launch traced here: 110 us
  Pallas kernels  99.7 us (90%)
  local copies, waits for them, and re-layouts  6.93 us (6%)
  other arithmetic  2.38 us (2%)
    pallas_call x1, Pallas kernels, attention(): pl.pallas_call(attend_kernel, out_shape=(jax.ShapeDtypeStruct(q.shape, bf...  96.5 us
    pallas_call x1, Pallas kernels, reordered(): pl.pallas_call(reorder_kernel, out_shape=jax.ShapeDtypeStruct(source.shap...  3.26 us

profile of v4, /device:TPU:0, one launch (start us, length us, event | category | flops | bytes accessed | tf_op | source)
XLA Modules:
  0.0 110.4 jit_solution(3261879725091909451)
XLA Ops:
  0.6 0.0 copy-start
  0.6 0.8 copy.23
  1.4 0.8 copy.25
  2.2 0.1 multiply_reduce_fusion
  2.3 1.5 %fusion.5.new_ref = bf16[8,8,640]{2,1,0:T(8,128)(2,1)} fusion(bf16[8,2,64]{2,1,0:T(2,128)(2,1)} %param.18, bf16[8,2,512]{2,1,0:T(2,128)(2,1)} %param.17), kind=kLoop, calls=%fused_computation.9 | loop fusion | flops 409600 | bytes 100352 | tf_op jit(solution)/shard_map/concatenate | solution.py:579
  3.8 0.9 fusion.14
  4.7 0.1 squeeze.19
  4.8 0.1 squeeze.20
  5.0 0.8 pad_maximum_fusion.krope_ref
  5.7 1.0 reshape.91
  6.8 0.2 convolution_convert_fusion
  6.9 0.7 reshape.92.blocks_ref
  7.6 0.0 copy-done
  7.6 0.2 copy.21
  7.7 0.5 reshape.89
  8.3 0.2 copy.22
  8.5 0.9 copy.24.rope_ref
  9.4 96.5 %shard_map.140 = (bf16[8,256,512]{2,1,0:T(8,128)(2,1)}, bf16[2,2,7168]{2,1,0:T(2,128)(2,1)}) custom-call(s32[8]{0:T(128)} %slot_ref.3, bf16[8,256,512]{2,1,0:T(8,128)(2,1)} %bitcast.22, bf16[8,128,128]{2,1,0:T(8,128)(2,1)} %copy.24.rope_ref, bf16[8,8,640]{2,1,0:T(8,128)(2,1)} %fusion.5.new_ref, bf16[1024,512]{1,0:T(8,128)(2,1)} %bitcast.27, ...), custom_call_target="tpu_custom_call" | custom-call | tf_op jit(solution)/shard_map/pallas_call | solution.py:434
  105.9 0.0 copy-start.1
  105.9 3.3 %shard_map.141 = bf16[8,256,512]{2,1,0:T(8,128)(2,1)} custom-call(s32[8]{0:T(128)} %slot_ref.3, bf16[8,256,512]{2,1,0:T(8,128)(2,1)} %get-tuple-element.4.source), custom_call_target="tpu_custom_call" | custom-call | tf_op jit(solution)/shard_map/pallas_call | solution.py:523
  109.1 0.0 copy-done.1
  109.1 0.5 fusion
  109.6 0.8 reshape.94
  (3 shorter events, 0.0 us)
Async XLA Ops:
  0.6 7.0 %copy-start = (bf16[8,2,8192]{2,1,0:T(2,128)(2,1)S(1)}, bf16[8,2,8192]{2,1,0:T(2,128)(2,1)}, u32[]{:S(2)}) copy-start(bf16[8,2,8192]{2,1,0:T(2,128)(2,1)} %param.16) | copy-start | bytes 786436
  105.9 3.3 %copy-start.1 = (bf16[2,2,7168]{2,1,0:T(2,128)(2,1)S(1)}, bf16[2,2,7168]{2,1,0:T(2,128)(2,1)}, u32[]{:S(2)}) copy-start(bf16[2,2,7168]{2,1,0:T(2,128)(2,1)} %get-tuple-element.5) | copy-start | bytes 172036
